TPU v7x, 32 devices: a whole 2x2x4 slice. The times are simulated.
32 devices in a mesh: gx: 4 (over x, core), gy: 8 (over z, y).
Axes of the slice: x: 2, y: 2, z: 4, core: 2. Of those that a mesh axis runs over, the one named last changes fastest.
Arguments:
- target_ids: int32 [2, 4, 512], P(None, 'gx', 'gy'), may hold values from 0 to 16383
- labels: int32 [2, 4, 512], P(None, 'gx', 'gy'), may hold values from 0 to 16383
- lengths: int32 [2, 4], replicated, may hold values from 128 to 512, as said below
- memory: bfloat16 [2, 4, 1024, 512], P(None, 'gx', 'gy'), may hold values from -6 to 6
- embedding: bfloat16 [16384, 512], P(('gx', 'gy')), may hold values from -6 to 6
- head: bfloat16 [16384, 512], P(('gx', 'gy')), may hold values from -0.5 to 0.5
- gain_self: bfloat16 [512], P(('gx', 'gy')), may hold values from 0.5 to 1.5
- w_query: bfloat16 [512, 384], P(('gx', 'gy')), may hold values from -0.0625 to 0.0625
- w_key: bfloat16 [512, 384], P(('gx', 'gy')), may hold values from -0.25 to 0.25
- w_value: bfloat16 [512, 384], P(('gx', 'gy')), may hold values from -0.25 to 0.25
- w_out: bfloat16 [512, 384], P(('gx', 'gy')), may hold values from -1.25 to 1.25
- relative_bias: bfloat16 [6, 32], replicated, may hold values from -4 to 4
- gain_cross: bfloat16 [512], P(('gx', 'gy')), may hold values from 0.5 to 1.5
- c_query: bfloat16 [512, 384], P(('gx', 'gy')), may hold values from -0.0625 to 0.0625
- c_key: bfloat16 [512, 384], P(('gx', 'gy')), may hold values from -0.25 to 0.25
- c_value: bfloat16 [512, 384], P(('gx', 'gy')), may hold values from -0.25 to 0.25
- c_out: bfloat16 [512, 384], P(('gx', 'gy')), may hold values from -1.25 to 1.25
- gain_ff: bfloat16 [512], P(('gx', 'gy')), may hold values from 0.5 to 1.5
- w_gate: bfloat16 [512, 1024], P(('gx', 'gy')), may hold values from -0.25 to 0.25
- w_up: bfloat16 [512, 1024], P(('gx', 'gy')), may hold values from -0.25 to 0.25
- w_down: bfloat16 [512, 1024], P(('gx', 'gy')), may hold values from -0.1875 to 0.1875
- gain_final: bfloat16 [512], P(('gx', 'gy')), may hold values from 0.5 to 1.5
Outputs:
- loss: float32 [], replicated
- memory_grad: float32 [2, 4, 1024, 512], P(None, 'gx', 'gy')
- embedding_grad: float32 [16384, 512], P(('gx', 'gy'))
- head_grad: float32 [16384, 512], P(('gx', 'gy'))
- gain_self_grad: float32 [512], P(('gx', 'gy'))
- w_query_grad: float32 [512, 384], P(('gx', 'gy'))
- w_key_grad: float32 [512, 384], P(('gx', 'gy'))
- w_value_grad: float32 [512, 384], P(('gx', 'gy'))
- w_out_grad: float32 [512, 384], P(('gx', 'gy'))
- rel_bias_grad: float32 [6, 32], replicated
- gain_cross_grad: float32 [512], P(('gx', 'gy'))
- c_query_grad: float32 [512, 384], P(('gx', 'gy'))
- c_key_grad: float32 [512, 384], P(('gx', 'gy'))
- c_value_grad: float32 [512, 384], P(('gx', 'gy'))
- c_out_grad: float32 [512, 384], P(('gx', 'gy'))
- gain_ff_grad: float32 [512], P(('gx', 'gy'))
- w_gate_grad: float32 [512, 1024], P(('gx', 'gy'))
- w_up_grad: float32 [512, 1024], P(('gx', 'gy'))
- w_down_grad: float32 [512, 1024], P(('gx', 'gy'))
- gain_final_grad: float32 [512], P(('gx', 'gy'))
Inputs may be any that keep to these rules, and one draw needn't show every extreme that they name: `lengths`: each sequence's count of live target positions; some sequence has all 512, some has a quarter of 512.
All inputs are finite; a program needn't handle non-finite values.
Results may differ from a plain program's by a relative error of at most 0.024.
The roundings to bfloat16 on the way count: a program that leaves them out, or rounds other values in their place, can miss the bound.
Values may be sent and summed in bfloat16 or wider, within the bound.
A program may use at most 320 MiB of HBM per device.

v0:
```python
import math

import jax
import jax.numpy as jnp
from jax import lax
from jax.sharding import PartitionSpec as P

HEADS = 6
HEAD = 64
BUCKETS = 32


eps = 1e-06
masked_score = -1000000000.0


def as_sent(array):
    return jax.tree.map(lambda a: a.astype(jnp.bfloat16) if a.dtype == jnp.float32 else a, array)


def joined(value, axis, join):
    pieces = jax.tree.map(lambda part: lax.all_gather(part, axis), value)
    head = jax.tree.map(lambda part: part[0], pieces)
    tail = jax.tree.map(lambda part: part[1:], pieces)
    running, _ = lax.scan(lambda running, piece: (join(running, piece), None), head, tail)
    return running


def bucket_edges():
    edges = []
    for target in range(1, 32):
        if target < 16:
            edges.append(target)
        else:
            found = 0
            for distance in range(16, 4096):
                value = 16 + int(math.log(distance / 16.0) / math.log(8.0) * 16.0)
                if found == 0 and value >= target:
                    found = distance
            edges.append(found)
    return edges


def bucket_of(distance):
    edges = jnp.array(bucket_edges(), dtype=jnp.int32)
    return jnp.sum((distance[..., None] >= edges).astype(jnp.int32), axis=-1)


def rms_norm(rows, gain):
    return rows * lax.rsqrt(jnp.mean(rows * rows, axis=-1, keepdims=True) + eps) * gain


def gelu_tanh(value):
    return (
        0.5
        * value
        * (1.0 + jnp.tanh(0.7978845608028654 * (value + 0.044715 * value * value * value)))
    )


def norm_back(rows, gain, slope):
    _, pullback = jax.vjp(rms_norm, rows, gain)
    return pullback(slope)


def project(rows, weight):
    return jnp.einsum("msd,df->msf", rows, weight, preferred_element_type=jnp.float32)


def project_back(slope, weight):
    return jnp.einsum("msf,df->msd", slope, weight, preferred_element_type=jnp.float32)


def weight_grad(rows, slope):
    return jnp.einsum("msd,msf->df", rows, slope, preferred_element_type=jnp.float32)


def split_heads(tensor):
    return tensor.reshape(tensor.shape[0], tensor.shape[1], HEADS, HEAD)


def attend_scores(query, keys, bias_vector, mask):
    scores = jnp.einsum(
        "mqhe,mkhe->mhqk", split_heads(query), split_heads(keys), preferred_element_type=jnp.float32
    )
    if bias_vector is not None:
        scores = scores + bias_vector[None]
    if mask is not None:
        scores = jnp.where(mask[:, None], scores, masked_score)
    return scores


def attend(query, keys, values, bias_vector, mask):
    scores = attend_scores(query, keys, bias_vector, mask)
    highest = jnp.max(scores, axis=-1, keepdims=True)
    log_total = highest + jnp.log(jnp.sum(jnp.exp(scores - highest), axis=-1, keepdims=True))
    shares = jnp.exp(scores - log_total).astype(jnp.bfloat16)
    output = jnp.einsum(
        "mhqk,mkhe->mqhe", shares, split_heads(values), preferred_element_type=jnp.float32
    )
    return (output.reshape(query.shape).astype(jnp.bfloat16), log_total)


def attend_back(query, keys, values, bias_vector, mask, log_total, out_slope):
    scores = attend_scores(query, keys, bias_vector, mask)
    shares = jnp.exp(scores - log_total)
    out_heads = split_heads(out_slope)
    share_slope = jnp.einsum(
        "mqhe,mkhe->mhqk", out_heads, split_heads(values), preferred_element_type=jnp.float32
    )
    inner = jnp.sum(shares * share_slope, axis=-1, keepdims=True)
    score_gradient = (shares * (share_slope - inner)).astype(jnp.bfloat16)
    query_slope = jnp.einsum(
        "mhqk,mkhe->mqhe", score_gradient, split_heads(keys), preferred_element_type=jnp.float32
    )
    key_slope = jnp.einsum(
        "mhqk,mqhe->mkhe", score_gradient, split_heads(query), preferred_element_type=jnp.float32
    )
    value_slope = jnp.einsum(
        "mhqk,mqhe->mkhe",
        shares.astype(jnp.bfloat16),
        out_heads,
        preferred_element_type=jnp.float32,
    )
    width = HEADS * HEAD
    return (
        query_slope.reshape(query.shape[0], query.shape[1], width),
        key_slope.reshape(keys.shape[0], keys.shape[1], width),
        value_slope.reshape(keys.shape[0], keys.shape[1], width),
        score_gradient,
    )


def join_totals(first, second):
    highest = jnp.maximum(first[0], second[0])
    spread = first[1] * jnp.exp(first[0] - highest) + second[1] * jnp.exp(second[0] - highest)
    return (highest, spread)


def share_keys(parts):
    return jax.tree.map(
        lambda part, own: part.astype(own.dtype),
        lax.all_gather(as_sent(parts), "gy", axis=1, tiled=True),
        parts,
    )


def scatter_keys(parts):
    return lax.psum_scatter(parts, "gy", scatter_dimension=1, tiled=True)


def position_rows(rows):
    return lax.all_gather(rows, "gx", axis=0, tiled=True)


def rows_back(rows):
    return lax.psum_scatter(rows, "gx", scatter_dimension=0, tiled=True)


def per_device(
    target_ids,
    labels,
    lengths,
    memory,
    embedding,
    head,
    gain_self,
    w_query,
    w_key,
    w_value,
    w_out,
    relative_bias,
    gain_cross,
    c_query,
    c_key,
    c_value,
    c_out,
    gain_ff,
    w_gate,
    w_up,
    w_down,
    gain_final,
):
    micro = target_ids.shape[0]
    seq_dev = target_ids.shape[2]
    width = embedding.shape[1]
    voc_dev = embedding.shape[0]
    tok_dev = micro * seq_dev
    n_gx = lax.axis_size("gx")
    n_gy = lax.axis_size("gy")
    column = lax.axis_index("gy")
    row_group = lax.axis_index("gx")
    span = n_gy * voc_dev
    rows_total = n_gx * tok_dev
    vocab_start = row_group * span
    own_ids = target_ids.reshape(tok_dev)
    own_labels = labels.reshape(tok_dev)
    grid_ids, grid_labels = (
        lax.all_gather(own_ids, "gx", axis=0, tiled=True),
        lax.all_gather(own_labels, "gx", axis=0, tiled=True),
    )
    embed_rows, head_rows = (
        lax.all_gather(embedding, "gy", axis=0, tiled=True),
        lax.all_gather(head, "gy", axis=0, tiled=True),
    )
    local_ids = grid_ids - vocab_start
    inside = (local_ids >= 0) & (local_ids < span)
    picked_rows = jnp.take(embed_rows, jnp.clip(local_ids, 0, span - 1), axis=0)
    partial_rows = jnp.where(inside[:, None], picked_rows.astype(jnp.float32), 0.0)
    embedded = rows_back(partial_rows)
    resid0 = embedded.reshape(micro, seq_dev, width)
    gathered = (
        lax.all_gather(gain_self, ("gx", "gy"), axis=0, tiled=True),
        lax.all_gather(w_query, ("gx", "gy"), axis=0, tiled=True),
        lax.all_gather(w_key, ("gx", "gy"), axis=0, tiled=True),
        lax.all_gather(w_value, ("gx", "gy"), axis=0, tiled=True),
        lax.all_gather(w_out, ("gx", "gy"), axis=0, tiled=True),
        lax.all_gather(gain_cross, ("gx", "gy"), axis=0, tiled=True),
        lax.all_gather(c_query, ("gx", "gy"), axis=0, tiled=True),
        lax.all_gather(c_key, ("gx", "gy"), axis=0, tiled=True),
        lax.all_gather(c_value, ("gx", "gy"), axis=0, tiled=True),
        lax.all_gather(c_out, ("gx", "gy"), axis=0, tiled=True),
        lax.all_gather(gain_ff, ("gx", "gy"), axis=0, tiled=True),
        lax.all_gather(w_gate, ("gx", "gy"), axis=0, tiled=True),
        lax.all_gather(w_up, ("gx", "gy"), axis=0, tiled=True),
        lax.all_gather(w_down, ("gx", "gy"), axis=0, tiled=True),
        lax.all_gather(gain_final, ("gx", "gy"), axis=0, tiled=True),
    )
    (
        norm_self,
        self_query,
        self_key,
        self_value,
        self_out,
        norm_cross,
        cross_query,
        cross_key,
        cross_value,
        cross_out,
        norm_ff,
        gate_full,
        up_full,
        down_full,
        norm_final,
    ) = gathered
    norm_self = norm_self.astype(jnp.float32)
    norm_cross = norm_cross.astype(jnp.float32)
    norm_ff = norm_ff.astype(jnp.float32)
    norm_final = norm_final.astype(jnp.float32)
    live_length = lax.dynamic_index_in_dim(lengths, row_group, axis=1, keepdims=False)
    query_pos = column * seq_dev + jnp.arange(seq_dev, dtype=jnp.int32)
    key_pos = jnp.arange(seq_dev * n_gy, dtype=jnp.int32)
    bucket = bucket_of(jnp.maximum(query_pos[:, None] - key_pos[None, :], 0))
    indicator_rows = (bucket[None] == jnp.arange(BUCKETS, dtype=jnp.int32)[:, None, None]).astype(
        jnp.bfloat16
    )
    bias_vector = jnp.einsum(
        "som,ns->nom", indicator_rows, relative_bias, preferred_element_type=jnp.float32
    )
    causal = (key_pos[None, :] <= query_pos[:, None])[None] & (
        key_pos[None, None, :] < live_length[:, None, None]
    )
    memory_own = memory.reshape(micro, memory.shape[2], width)
    memory_keys = project(memory_own, cross_key).astype(jnp.bfloat16)
    memory_values = project(memory_own, cross_value).astype(jnp.bfloat16)
    normed_self = rms_norm(resid0, norm_self).astype(jnp.bfloat16)
    query_self = project(normed_self, self_query).astype(jnp.bfloat16)
    key_own = project(normed_self, self_key).astype(jnp.bfloat16)
    value_own = project(normed_self, self_value).astype(jnp.bfloat16)
    keys_self, values_self, keys_cross, values_cross = share_keys(
        (key_own, value_own, memory_keys, memory_values)
    )
    attn_self, total_self = attend(query_self, keys_self, values_self, bias_vector, causal)
    resid1 = resid0 + project_back(attn_self, self_out)
    normed_cross = rms_norm(resid1, norm_cross).astype(jnp.bfloat16)
    query_cross = project(normed_cross, cross_query).astype(jnp.bfloat16)
    attn_cross, total_cross = attend(query_cross, keys_cross, values_cross, None, None)
    resid2 = resid1 + project_back(attn_cross, cross_out)
    normed_ff = rms_norm(resid2, norm_ff).astype(jnp.bfloat16)
    gate_value = project(normed_ff, gate_full)
    up_value = project(normed_ff, up_full)
    hidden = (gelu_tanh(gate_value) * up_value).astype(jnp.bfloat16)
    resid3 = resid2 + project_back(hidden, down_full)
    final_rows = rms_norm(resid3, norm_final).astype(jnp.bfloat16)
    states = position_rows(final_rows.reshape(tok_dev, width))
    index = jnp.arange(rows_total, dtype=jnp.int32)
    owner = index // tok_dev
    batch_of = index % tok_dev // seq_dev
    place = column * seq_dev + index % seq_dev
    alive = (place < lengths[batch_of, owner]).astype(jnp.float32)
    targets = grid_labels - vocab_start
    block = math.gcd(rows_total, 512)
    count_blocks = rows_total // block
    state_blocks = states.reshape(count_blocks, block, width)
    target_blocks = targets.reshape(count_blocks, block)
    columns = jnp.arange(span, dtype=jnp.int32)

    def forward_block(carry, pieces):
        rows, goal = pieces
        logits = jnp.einsum("rd,vd->rv", rows, head_rows, preferred_element_type=jnp.float32)
        highest = jnp.max(logits, axis=1)
        spread = jnp.sum(jnp.exp(logits - highest[:, None]), axis=1)
        picked = jnp.sum(jnp.where(columns[None, :] == goal[:, None], logits, 0.0), axis=1)
        return (carry, (logits, highest, spread, picked))

    _, (logit_blocks, highest, spread, picked) = lax.scan(
        forward_block, jnp.zeros((), jnp.float32), (state_blocks, target_blocks)
    )
    highest, spread = joined(
        (highest.reshape(rows_total), spread.reshape(rows_total)), "gx", join_totals
    )
    log_total = highest + jnp.log(spread)
    loss_part = jnp.where(row_group == 0, jnp.sum(alive * log_total), 0.0) - jnp.sum(
        alive * picked.reshape(rows_total)
    )

    def backward_block(carry, pieces):
        logits, rows, goal, alive_rows, totals = pieces
        hit = (columns[None, :] == goal[:, None]).astype(jnp.float32)
        slope = ((jnp.exp(logits - totals[:, None]) - hit) * alive_rows[:, None]).astype(
            jnp.bfloat16
        )
        carry = carry + jnp.einsum("rv,rd->vd", slope, rows, preferred_element_type=jnp.float32)
        partial_sum = jnp.einsum("rv,vd->rd", slope, head_rows, preferred_element_type=jnp.float32)
        return (carry, partial_sum)

    head_portion, partial_blocks = lax.scan(
        backward_block,
        jnp.zeros((span, width), jnp.float32),
        (
            logit_blocks,
            state_blocks,
            target_blocks,
            alive.reshape(count_blocks, block),
            log_total.reshape(count_blocks, block),
        ),
    )
    final_slope = rows_back(partial_blocks.reshape(rows_total, width))
    final_slope = final_slope.reshape(micro, seq_dev, width)
    grad3, norm_final_grad = norm_back(resid3, norm_final, final_slope)
    down_in = grad3.astype(jnp.bfloat16)
    down_grad = weight_grad(down_in, hidden)
    hidden_slope = project(down_in, down_full)
    activated, gelu_pull = jax.vjp(gelu_tanh, gate_value)
    up_slope = (hidden_slope * activated).astype(jnp.bfloat16)
    gate_slope = gelu_pull(hidden_slope * up_value)[0].astype(jnp.bfloat16)
    gate_grad = weight_grad(normed_ff, gate_slope)
    up_gradient = weight_grad(normed_ff, up_slope)
    normed_slope = project_back(gate_slope, gate_full) + project_back(up_slope, up_full)
    back_part, norm_ff_grad = norm_back(resid2, norm_ff, normed_slope)
    grad2 = grad3 + back_part
    cross_in = grad2.astype(jnp.bfloat16)
    cross_out_grad = weight_grad(cross_in, attn_cross)
    attn_slope = project(cross_in, cross_out).astype(jnp.bfloat16)
    cross_query_slope, cross_key_slope, cross_value_slope, _ = attend_back(
        query_cross, keys_cross, values_cross, None, None, total_cross, attn_slope
    )
    cross_query_slope = cross_query_slope.astype(jnp.bfloat16)
    cross_query_grad = weight_grad(normed_cross, cross_query_slope)
    back_part, norm_cross_grad = norm_back(
        resid1, norm_cross, project_back(cross_query_slope, cross_query)
    )
    grad1 = grad2 + back_part
    self_in = grad1.astype(jnp.bfloat16)
    self_out_grad = weight_grad(self_in, attn_self)
    attn_slope = project(self_in, self_out).astype(jnp.bfloat16)
    query_slope, key_slope, value_slope, score_gradient = attend_back(
        query_self, keys_self, values_self, bias_vector, causal, total_self, attn_slope
    )
    bias_gradient = jnp.einsum(
        "ovcj,ecj->ve", score_gradient, indicator_rows, preferred_element_type=jnp.float32
    )
    mem_key_slope, mem_value_slope, key_slope, value_slope = scatter_keys(
        (cross_key_slope, cross_value_slope, key_slope, value_slope)
    )
    mem_key_slope = mem_key_slope.astype(jnp.bfloat16)
    mem_value_slope = mem_value_slope.astype(jnp.bfloat16)
    cross_key_grad = weight_grad(memory_own, mem_key_slope)
    cross_value_grad = weight_grad(memory_own, mem_value_slope)
    memory_grad = project_back(mem_key_slope, cross_key) + project_back(
        mem_value_slope, cross_value
    )
    key_slope = key_slope.astype(jnp.bfloat16)
    value_slope = value_slope.astype(jnp.bfloat16)
    query_slope = query_slope.astype(jnp.bfloat16)
    self_query_grad = weight_grad(normed_self, query_slope)
    self_key_grad = weight_grad(normed_self, key_slope)
    self_value_grad = weight_grad(normed_self, value_slope)
    normed_slope = (
        project_back(query_slope, self_query)
        + project_back(key_slope, self_key)
        + project_back(value_slope, self_value)
    )
    back_part, norm_self_grad = norm_back(resid0, norm_self, normed_slope)
    grad0 = grad1 + back_part
    grid_slopes = position_rows(grad0.reshape(tok_dev, width).astype(jnp.bfloat16))
    segment = jnp.where(inside, local_ids, span)
    embed_part = jax.ops.segment_sum(
        grid_slopes.astype(jnp.float32), segment, num_segments=span + 1
    )[:span]
    embedding_grad, head_grad = (
        lax.psum_scatter(embed_part, "gy", scatter_dimension=0, tiled=True),
        lax.psum_scatter(head_portion, "gy", scatter_dimension=0, tiled=True),
    )
    sums = (
        lax.psum_scatter(norm_self_grad, ("gx", "gy"), scatter_dimension=0, tiled=True),
        lax.psum_scatter(self_query_grad, ("gx", "gy"), scatter_dimension=0, tiled=True),
        lax.psum_scatter(self_key_grad, ("gx", "gy"), scatter_dimension=0, tiled=True),
        lax.psum_scatter(self_value_grad, ("gx", "gy"), scatter_dimension=0, tiled=True),
        lax.psum_scatter(self_out_grad, ("gx", "gy"), scatter_dimension=0, tiled=True),
        lax.psum_scatter(norm_cross_grad, ("gx", "gy"), scatter_dimension=0, tiled=True),
        lax.psum_scatter(cross_query_grad, ("gx", "gy"), scatter_dimension=0, tiled=True),
        lax.psum_scatter(cross_key_grad, ("gx", "gy"), scatter_dimension=0, tiled=True),
        lax.psum_scatter(cross_value_grad, ("gx", "gy"), scatter_dimension=0, tiled=True),
        lax.psum_scatter(cross_out_grad, ("gx", "gy"), scatter_dimension=0, tiled=True),
        lax.psum_scatter(norm_ff_grad, ("gx", "gy"), scatter_dimension=0, tiled=True),
        lax.psum_scatter(gate_grad, ("gx", "gy"), scatter_dimension=0, tiled=True),
        lax.psum_scatter(up_gradient, ("gx", "gy"), scatter_dimension=0, tiled=True),
        lax.psum_scatter(down_grad, ("gx", "gy"), scatter_dimension=0, tiled=True),
        lax.psum_scatter(norm_final_grad, ("gx", "gy"), scatter_dimension=0, tiled=True),
    )
    bias_total, loss_total = lax.psum((bias_gradient, loss_part), ("gx", "gy"))
    loss = loss_total / jnp.sum(lengths).astype(jnp.float32)
    memory_out = memory_grad.reshape(micro, 1, memory.shape[2], width)
    return (
        loss,
        memory_out,
        embedding_grad,
        head_grad,
        sums[0],
        sums[1],
        sums[2],
        sums[3],
        sums[4],
        bias_total,
        sums[5],
        sums[6],
        sums[7],
        sums[8],
        sums[9],
        sums[10],
        sums[11],
        sums[12],
        sums[13],
        sums[14],
    )


def solution(mesh):
    placed = (
        P(None, "gx", "gy"),
        P(None, "gx", "gy"),
        P(),
        P(None, "gx", "gy", None),
        P(("gx", "gy"), None),
        P(("gx", "gy"), None),
        P(("gx", "gy")),
        P(("gx", "gy"), None),
        P(("gx", "gy"), None),
        P(("gx", "gy"), None),
        P(("gx", "gy"), None),
        P(),
        P(("gx", "gy")),
        P(("gx", "gy"), None),
        P(("gx", "gy"), None),
        P(("gx", "gy"), None),
        P(("gx", "gy"), None),
        P(("gx", "gy")),
        P(("gx", "gy"), None),
        P(("gx", "gy"), None),
        P(("gx", "gy"), None),
        P(("gx", "gy")),
    )
    return jax.shard_map(
        per_device,
        mesh=mesh,
        in_specs=placed,
        out_specs=(
            P(),
            P(None, "gx", "gy", None),
            P(("gx", "gy"), None),
            P(("gx", "gy"), None),
            P(("gx", "gy")),
            P(("gx", "gy"), None),
            P(("gx", "gy"), None),
            P(("gx", "gy"), None),
            P(("gx", "gy"), None),
            P(),
            P(("gx", "gy")),
            P(("gx", "gy"), None),
            P(("gx", "gy"), None),
            P(("gx", "gy"), None),
            P(("gx", "gy"), None),
            P(("gx", "gy")),
            P(("gx", "gy"), None),
            P(("gx", "gy"), None),
            P(("gx", "gy"), None),
            P(("gx", "gy")),
        ),
        check_vma=False,
    )
```

profile of v0, /device:TPU:0, one launch (start us, length us, event | category | flops | bytes accessed | tf_op | source)
XLA Modules:
  0.0 2655.2 jit_solution(1897883187788334507)
XLA Ops:
  8.0 76.7 %all_gather.90 = bf16[512,384]{1,0:T(8,128)(2,1)S(1)} all-gather(bf16[16,384]{1,0:T(8,128)(2,1)} %param.40), channel_id=1, replica_groups=mesh['gx'=4,'gy'=8] {'gx','gy'}, dimensions={0}, use_global_device_ids=true | all-gather | bytes 405504 | tf_op jit(solution)/shard_map/all_gather | solution.py:221
  86.5 67.5 %all_gather.94 = bf16[512,384]{1,0:T(8,128)(2,1)S(1)} all-gather(bf16[16,384]{1,0:T(8,128)(2,1)} %param.39), channel_id=1, replica_groups=mesh['gx'=4,'gy'=8] {'gx','gy'}, dimensions={0}, use_global_device_ids=true | all-gather | bytes 405504 | tf_op jit(solution)/shard_map/all_gather | solution.py:220
  157.1 5.0 all-gather.2
  162.8 4.7 gather_fusion.1
  171.8 4.8 gather_fusion
  177.1 68.6 %all_gather.84 = bf16[512,384]{1,0:T(8,128)(2,1)S(1)} all-gather(bf16[16,384]{1,0:T(8,128)(2,1)S(1)} %copy-done.96), channel_id=1, replica_groups=mesh['gx'=4,'gy'=8] {'gx','gy'}, dimensions={0}, use_global_device_ids=true | all-gather | bytes 405504 | tf_op jit(solution)/shard_map/all_gather | solution.py:216
  245.8 65.8 %all_gather.86 = bf16[512,384]{1,0:T(8,128)(2,1)S(1)} all-gather(bf16[16,384]{1,0:T(8,128)(2,1)S(1)} %copy-done.97), channel_id=1, replica_groups=mesh['gx'=4,'gy'=8] {'gx','gy'}, dimensions={0}, use_global_device_ids=true | all-gather | bytes 405504 | tf_op jit(solution)/shard_map/all_gather | solution.py:214
  311.6 68.4 %all_gather.87 = bf16[512,384]{1,0:T(8,128)(2,1)S(1)} all-gather(bf16[16,384]{1,0:T(8,128)(2,1)S(1)} %copy-done.98), channel_id=1, replica_groups=mesh['gx'=4,'gy'=8] {'gx','gy'}, dimensions={0}, use_global_device_ids=true | all-gather | bytes 405504 | tf_op jit(solution)/shard_map/all_gather | solution.py:215
  380.3 69.2 %all_gather.89 = bf16[512,384]{1,0:T(8,128)(2,1)S(1)} all-gather(bf16[16,384]{1,0:T(8,128)(2,1)S(1)} %copy-done.99), channel_id=1, replica_groups=mesh['gx'=4,'gy'=8] {'gx','gy'}, dimensions={0}, use_global_device_ids=true | all-gather | bytes 405504 | tf_op jit(solution)/shard_map/all_gather | solution.py:217
  449.5 68.4 %all_gather.93 = bf16[512,384]{1,0:T(8,128)(2,1)S(1)} all-gather(bf16[16,384]{1,0:T(8,128)(2,1)S(1)} %copy-done.100), channel_id=1, replica_groups=mesh['gx'=4,'gy'=8] {'gx','gy'}, dimensions={0}, use_global_device_ids=true | all-gather | bytes 405504 | tf_op jit(solution)/shard_map/all_gather | solution.py:219
  518.6 5.0 all-gather.5
  525.5 71.4 %all_gather.96 = bf16[512,384]{1,0:T(8,128)(2,1)} all-gather(bf16[16,384]{1,0:T(8,128)(2,1)S(1)} %copy-done.101), channel_id=1, replica_groups=mesh['gx'=4,'gy'=8] {'gx','gy'}, dimensions={0}, use_global_device_ids=true | all-gather | bytes 405504 | tf_op jit(solution)/shard_map/all_gather | solution.py:222
  597.9 36.9 %all-reduce.9 = (bf16[512]{0:T(512)(128)(2,1)S(1)}, bf16[512]{0:T(512)(128)(2,1)S(1)}, bf16[512]{0:T(512)(128)(2,1)S(1)}, bf16[512]{0:T(512)(128)(2,1)S(1)}) all-reduce(bf16[512]{0:T(512)(128)(2,1)S(1)} %dynamic-update-slice, bf16[512]{0:T(512)(128)(2,1)S(1)} %dynamic-update-slice.1, ...), channel_id=1, replica_groups=mesh['gx'=4,'gy'=8] {'gx','gy'}, use_global_device_ids=true, to_apply=%add | all-reduce | flops 2048 | bytes 8192
  637.9 2.6 copy.137
  640.5 2.6 copy.138
  646.7 32.3 %all_gather.85 = bf16[2,512,384]{2,1,0:T(8,128)(2,1)S(1)} all-gather(bf16[2,64,384]{2,1,0:T(8,128)(2,1)S(1)} %convolution_convert_fusion.11), channel_id=1, replica_groups=mesh['gx'=4,'gy'=8] {'gy'}, dimensions={1}, use_global_device_ids=true | all-gather | bytes 884736 | tf_op jit(solution)/shard_map/all_gather | solution.py:143
  680.6 32.3 %all_gather.88 = bf16[2,512,384]{2,1,0:T(8,128)(2,1)S(1)} all-gather(bf16[2,64,384]{2,1,0:T(8,128)(2,1)S(1)} %convolution_convert_fusion.9), channel_id=1, replica_groups=mesh['gx'=4,'gy'=8] {'gy'}, dimensions={1}, use_global_device_ids=true | all-gather | bytes 884736 | tf_op jit(solution)/shard_map/all_gather | solution.py:143
  713.2 2.0 fusion.93
  719.0 2.3 fusion.94
  725.4 2.4 fusion.19
  727.8 2.6 multiply_convert_fusion.4
  733.2 8.3 all_gather.102
  741.5 4.8 fusion.95
  746.3 5.2 all-gather.3
  751.5 3.4 select_reduce_fusion
  754.9 5.6 all-gather.4
  762.3 6.0 while.2
  769.6 5.5 multiply_convert_fusion
  775.1 2.0 copy-done.5
  777.1 3.3 fusion.96
  780.5 23.7 reduce-scatter.26.cloned.1.call-done
  806.9 2.5 multiply_convert_fusion.3
  814.6 2.4 multiply_reduce_fusion
  824.4 2.4 multiply_reduce_fusion.1
  830.3 3.1 copy.150
  833.5 3.1 fusion.59
  836.6 3.0 copy.152
  839.8 3.9 fusion.97
  843.7 3.3 fusion.29
  852.3 2.3 convolution_bitcast_fusion.6
  856.0 43.2 %reduce-scatter.32.cloned.1.call-done = f32[2,64,384]{2,1,0:T(8,128)} async-done(((f32[2,512,384]{2,1,0:T(8,128)}), f32[2,64,384]{2,1,0:T(8,128)}) %reduce-scatter.32.cloned.1.call-update) | async-done | bytes 196624 | tf_op jit(solution)/shard_map/reduce_scatter | solution.py:149
  899.2 2.1 convolution_bitcast_fusion.9
  901.4 65.9 %reduce-scatter.34.cloned.1.call-done = f32[2,64,384]{2,1,0:T(8,128)} async-done(((f32[2,512,384]{2,1,0:T(8,128)}), f32[2,64,384]{2,1,0:T(8,128)}) %reduce-scatter.34.cloned.1.call-update) | async-done | bytes 196624 | tf_op jit(solution)/shard_map/reduce_scatter | solution.py:149
  967.3 2.1 convolution_bitcast_fusion.8
  975.3 69.2 %reduce-scatter.28.cloned.1.call-done = f32[2,128,384]{1,2,0:T(8,128)} async-done(((f32[2,1024,384]{1,2,0:T(8,128)}), f32[2,128,384]{1,2,0:T(8,128)}) %reduce-scatter.28.cloned.1.call-update) | async-done | bytes 393232 | tf_op jit(solution)/shard_map/reduce_scatter | solution.py:149
  1047.0 75.1 %reduce-scatter.30.cloned.1.call-done = f32[2,128,384]{1,2,0:T(8,128)} async-done(((f32[2,1024,384]{1,2,0:T(8,128)}), f32[2,128,384]{1,2,0:T(8,128)}) %reduce-scatter.30.cloned.1.call-update) | async-done | bytes 393232 | tf_op jit(solution)/shard_map/reduce_scatter | solution.py:149
  1124.6 7.9 fusion.99
  1134.7 7.1 all_gather.107
  1141.8 7.8 scatter_custom_fusion
  1149.6 7.7 slice.36
  1161.1 39.5 %all-reduce.8 = (f32[]{:T(128)}, f32[512]{0:T(512)S(1)}, f32[6,32]{1,0:T(8,128)}, f32[512]{0:T(512)S(1)}, f32[512]{0:T(512)S(1)}, /*index=5*/f32[512]{0:T(512)S(1)}) all-reduce(f32[]{:T(128)S(6)} %sub.145, f32[512]{0:T(512)S(1)} %get-tuple-element.195, f32[6,32]{1,0:T(8,128)S(1)} %fusion.10, ...), channel_id=1, replica_groups=mesh['gx'=4,'gy'=8] {'gx','gy'}, use_global_device_ids=true, to_apply=%region_17.18 | all-reduce | flops 2241 | bytes 17928 | tf_op jit(solution)/shard_map/psum | solution.py:422
  1205.1 18.1 reduce-scatter.40.cloned.1.call-done
  1223.2 100.8 %reduce-scatter.46.cloned.1.call-done = f32[16,384]{1,0:T(8,128)} async-done(((f32[512,384]{1,0:T(8,128)}), f32[16,384]{1,0:T(8,128)}) %reduce-scatter.46.cloned.1.call-update) | async-done | bytes 24592 | tf_op jit(solution)/shard_map/reduce_scatter | solution.py:410
  1324.0 100.8 %reduce-scatter.48.cloned.1.call-done = f32[16,384]{1,0:T(8,128)} async-done(((f32[512,384]{1,0:T(8,128)}), f32[16,384]{1,0:T(8,128)}) %reduce-scatter.48.cloned.1.call-update) | async-done | bytes 24592 | tf_op jit(solution)/shard_map/reduce_scatter | solution.py:412
  1424.9 100.8 %reduce-scatter.50.cloned.1.call-done = f32[16,384]{1,0:T(8,128)} async-done(((f32[512,384]{1,0:T(8,128)}), f32[16,384]{1,0:T(8,128)}) %reduce-scatter.50.cloned.1.call-update) | async-done | bytes 24592 | tf_op jit(solution)/shard_map/reduce_scatter | solution.py:415
  1525.7 100.8 %reduce-scatter.42.cloned.1.call-done = f32[16,384]{1,0:T(8,128)} async-done(((f32[512,384]{1,0:T(8,128)}), f32[16,384]{1,0:T(8,128)}) %reduce-scatter.42.cloned.1.call-update) | async-done | bytes 24592 | tf_op jit(solution)/shard_map/reduce_scatter | solution.py:408
  1626.5 101.0 %reduce-scatter.44.cloned.1.call-done = f32[16,384]{1,0:T(8,128)} async-done(((f32[512,384]{1,0:T(8,128)}), f32[16,384]{1,0:T(8,128)}) %reduce-scatter.44.cloned.1.call-update) | async-done | bytes 24592 | tf_op jit(solution)/shard_map/reduce_scatter | solution.py:409
  1727.5 141.4 %reduce-scatter.52.cloned.1.call-done = f32[16,1024]{1,0:T(8,128)} async-done(((f32[512,1024]{1,0:T(8,128)}), f32[16,1024]{1,0:T(8,128)}) %reduce-scatter.52.cloned.1.call-update) | async-done | bytes 65552 | tf_op jit(solution)/shard_map/reduce_scatter | solution.py:417
  1868.9 138.4 %reduce-scatter.54.cloned.1.call-done = f32[16,1024]{1,0:T(8,128)} async-done(((f32[512,1024]{1,0:T(8,128)}), f32[16,1024]{1,0:T(8,128)}) %reduce-scatter.54.cloned.1.call-update) | async-done | bytes 65552 | tf_op jit(solution)/shard_map/reduce_scatter | solution.py:418
  2007.3 139.3 %reduce-scatter.56.cloned.1.call-done = f32[16,1024]{1,0:T(8,128)} async-done(((f32[512,1024]{1,0:T(8,128)}), f32[16,1024]{1,0:T(8,128)}) %reduce-scatter.56.cloned.1.call-update) | async-done | bytes 65552 | tf_op jit(solution)/shard_map/reduce_scatter | solution.py:419
  2146.6 98.4 %reduce-scatter.58.cloned.1.call-done = f32[16,384]{1,0:T(8,128)} async-done(((f32[512,384]{1,0:T(8,128)}), f32[16,384]{1,0:T(8,128)}) %reduce-scatter.58.cloned.1.call-update) | async-done | bytes 24592
  2245.1 100.9 %reduce-scatter.60.cloned.1.call-done = f32[16,384]{1,0:T(8,128)} async-done(((f32[512,384]{1,0:T(8,128)}), f32[16,384]{1,0:T(8,128)}) %reduce-scatter.60.cloned.1.call-update) | async-done | bytes 24592
  2345.9 150.8 %reduce-scatter.38.cloned.1.call-done = f32[512,512]{1,0:T(8,128)} async-done(((f32[4096,512]{1,0:T(8,128)}), f32[512,512]{1,0:T(8,128)}) %reduce-scatter.38.cloned.1.call-update) | async-done | bytes 1048592 | tf_op jit(solution)/shard_map/reduce_scatter | solution.py:403
  2496.7 150.7 %reduce-scatter.36.cloned.1.call-done = f32[512,512]{1,0:T(8,128)} async-done(((f32[4096,512]{1,0:T(8,128)}), f32[512,512]{1,0:T(8,128)}) %reduce-scatter.36.cloned.1.call-update) | async-done | bytes 1048592 | tf_op jit(solution)/shard_map/reduce_scatter | solution.py:402
  (423 shorter events, 86.3 us)
Async XLA Ops:
  7.2 78.3 %copy-start = (bf16[2,1,128,512]{3,2,1,0:T(8,128)(2,1)S(1)}, bf16[2,1,128,512]{3,2,1,0:T(8,128)(2,1)}, u32[]{:S(2)}) copy-start(bf16[2,1,128,512]{3,2,1,0:T(8,128)(2,1)} %param.28) | copy-start | bytes 786436
  7.2 149.1 %copy-start.115 = (s32[2,1,64]{2,1,0:T(1,128)S(1)}, s32[2,1,64]{2,1,0:T(1,128)}, u32[]{:S(2)}) copy-start(s32[2,1,64]{2,1,0:T(1,128)} %param.25) | copy-start | bytes 1540
  7.2 155.6 %all-gather.14.cloned.1.call-start = ((), (), s32[]{:S(2)}) async-start(), calls=%async_computation.19 | async-start | bytes 4718592 | tf_op jit(solution)/shard_map/all_gather | solution.py:203
  8.0 630.0 %all-gather.16.cloned.1.call-start = ((), (), s32[]{:S(2)}) async-start(), calls=%async_computation.21 | async-start | bytes 1769472 | tf_op jit(solution)/shard_map/all_gather | solution.py:143
  86.5 554.0 %all-gather.18.cloned.1.call-start = ((), (), s32[]{:S(2)}) async-start(), calls=%async_computation.22 | async-start | bytes 1769472 | tf_op jit(solution)/shard_map/all_gather | solution.py:143
  155.8 487.3 %reduce-scatter.24.cloned.1.call-start = ((), (), s32[]{:S(2)}) async-start(), calls=%async_computation.20 | async-start | bytes 1310720 | tf_op jit(solution)/shard_map/reduce_scatter | solution.py:157
  162.8 9.0 copy-start.1
  167.5 9.6 copy-start.96
  167.5 78.3 %copy-start.97 = (bf16[16,384]{1,0:T(8,128)(2,1)S(1)}, bf16[16,384]{1,0:T(8,128)(2,1)}, u32[]{:S(2)}) copy-start(bf16[16,384]{1,0:T(8,128)(2,1)} %param.32) | copy-start | bytes 36868
  167.5 144.1 %copy-start.98 = (bf16[16,384]{1,0:T(8,128)(2,1)S(1)}, bf16[16,384]{1,0:T(8,128)(2,1)}, u32[]{:S(2)}) copy-start(bf16[16,384]{1,0:T(8,128)(2,1)} %param.33) | copy-start | bytes 36868
  167.6 212.7 %copy-start.99 = (bf16[16,384]{1,0:T(8,128)(2,1)S(1)}, bf16[16,384]{1,0:T(8,128)(2,1)}, u32[]{:S(2)}) copy-start(bf16[16,384]{1,0:T(8,128)(2,1)} %param.35) | copy-start | bytes 36868
  168.7 280.7 %copy-start.100 = (bf16[16,384]{1,0:T(8,128)(2,1)S(1)}, bf16[16,384]{1,0:T(8,128)(2,1)}, u32[]{:S(2)}) copy-start(bf16[16,384]{1,0:T(8,128)(2,1)} %param.38) | copy-start | bytes 36868
  168.7 349.1 %copy-start.116 = (s32[2,1,64]{2,1,0:T(1,128)S(1)}, s32[2,1,64]{2,1,0:T(1,128)}, u32[]{:S(2)}) copy-start(s32[2,1,64]{2,1,0:T(1,128)} %param.26) | copy-start | bytes 1540
  168.7 355.5 %copy-start.118 = (s32[31]{0:T(128)S(1)}, s32[31]{0:T(128)}, u32[]{:S(2)}) copy-start(s32[31]{0:T(128)} %constant.165.clone) | copy-start | bytes 376
  168.8 356.0 %copy-start.114 = (bf16[6,32]{1,0:T(8,128)(2,1)S(1)}, bf16[6,32]{1,0:T(8,128)(2,1)}, u32[]{:S(2)}) copy-start(bf16[6,32]{1,0:T(8,128)(2,1)} %param.36) | copy-start | bytes 1156
  168.8 556.7 %all-gather.20.cloned.1.call-start = ((), (), s32[]{:S(2)}) async-start(), calls=%async_computation.23 | async-start | bytes 1081344 | tf_op jit(solution)/shard_map/all_gather | solution.py:224
  169.4 558.5 %all-gather.22.cloned.1.call-start = ((), (), s32[]{:S(2)}) async-start(), calls=%async_computation.24 | async-start | bytes 1081344 | tf_op jit(solution)/shard_map/all_gather | solution.py:225
  169.9 560.5 %all-gather.24.cloned.1.call-start = ((), (), s32[]{:S(2)}) async-start(), calls=%async_computation.25 | async-start | bytes 1081344 | tf_op jit(solution)/shard_map/all_gather | solution.py:226
  170.7 570.8 %all-gather.26.cloned.1.call-start = ((), (), s32[]{:S(2)}) async-start(), calls=%async_computation.26 | async-start | bytes 4718592 | tf_op jit(solution)/shard_map/all_gather | solution.py:204
  171.4 354.0 %copy-start.101 = (bf16[16,384]{1,0:T(8,128)(2,1)S(1)}, bf16[16,384]{1,0:T(8,128)(2,1)}, u32[]{:S(2)}) copy-start(bf16[16,384]{1,0:T(8,128)(2,1)} %param.41) | copy-start | bytes 36868
  171.5 632.7 %reduce-scatter.26.cloned.1.call-start = ((), (), s32[]{:S(2)}) async-start(), calls=%async_computation.27 | async-start | bytes 1310720 | tf_op jit(solution)/shard_map/reduce_scatter | solution.py:157
  171.7 425.2 %copy-start.119 = (bf16[16]{0:T(256)(128)(2,1)S(1)}, bf16[16]{0:T(256)(128)(2,1)}, u32[]{:S(2)}) copy-start(bf16[16]{0:T(256)(128)(2,1)} %param.31) | copy-start | bytes 100
  171.7 425.4 %copy-start.120 = (bf16[16]{0:T(256)(128)(2,1)S(1)}, bf16[16]{0:T(256)(128)(2,1)}, u32[]{:S(2)}) copy-start(bf16[16]{0:T(256)(128)(2,1)} %param.37) | copy-start | bytes 100
  171.8 425.6 %copy-start.121 = (bf16[16]{0:T(256)(128)(2,1)S(1)}, bf16[16]{0:T(256)(128)(2,1)}, u32[]{:S(2)}) copy-start(bf16[16]{0:T(256)(128)(2,1)} %param.42) | copy-start | bytes 100
  171.8 425.9 %copy-start.122 = (bf16[16]{0:T(256)(128)(2,1)S(1)}, bf16[16]{0:T(256)(128)(2,1)}, u32[]{:S(2)}) copy-start(bf16[16]{0:T(256)(128)(2,1)} %param.46) | copy-start | bytes 100
  245.8 400.6 %copy-start.42 = (bf16[512,384]{1,0:T(8,128)(2,1)}, bf16[512,384]{1,0:T(8,128)(2,1)S(1)}, u32[]{:S(2)}) copy-start(bf16[512,384]{1,0:T(8,128)(2,1)S(1)} %all_gather.84) | copy-start | bytes 1179652
  311.6 367.7 %copy-start.46 = (bf16[512,384]{1,0:T(8,128)(2,1)}, bf16[512,384]{1,0:T(8,128)(2,1)S(1)}, u32[]{:S(2)}) copy-start(bf16[512,384]{1,0:T(8,128)(2,1)S(1)} %all_gather.86) | copy-start | bytes 1179652
  380.0 300.3 %copy-start.44 = (bf16[512,384]{1,0:T(8,128)(2,1)}, bf16[512,384]{1,0:T(8,128)(2,1)S(1)}, u32[]{:S(2)}) copy-start(bf16[512,384]{1,0:T(8,128)(2,1)S(1)} %all_gather.87) | copy-start | bytes 1179652
  449.5 267.3 %copy-start.36 = (bf16[512,384]{1,0:T(8,128)(2,1)}, bf16[512,384]{1,0:T(8,128)(2,1)S(1)}, u32[]{:S(2)}) copy-start(bf16[512,384]{1,0:T(8,128)(2,1)S(1)} %all_gather.89) | copy-start | bytes 1179652
  517.8 199.9 %copy-start.48 = (bf16[512,384]{1,0:T(8,128)(2,1)}, bf16[512,384]{1,0:T(8,128)(2,1)S(1)}, u32[]{:S(2)}) copy-start(bf16[512,384]{1,0:T(8,128)(2,1)S(1)} %all_gather.93) | copy-start | bytes 1179652
  524.7 115.8 %copy-start.70 = (s32[64,512]{1,0:T(8,128)}, s32[64,512]{1,0:T(8,128)S(1)}, u32[]{:S(2)}) copy-start(s32[64,512]{1,0:T(8,128)S(1)} %convert_reduce_fusion) | copy-start | bytes 393220
  634.7 10.1 copy-start.76
  636.1 81.7 %copy-start.78 = (f32[512]{0:T(512)}, f32[512]{0:T(512)S(1)}, u32[]{:S(2)}) copy-start(f32[512]{0:T(512)S(1)} %convert_element_type.180) | copy-start | bytes 6148
  645.4 67.8 %copy-start.94 = (f32[2,64]{1,0:T(2,128)}, f32[2,64]{1,0:T(2,128)S(1)}, u32[]{:S(2)}) copy-start(f32[2,64]{1,0:T(2,128)S(1)} %rsqrt.47) | copy-start | bytes 1540
  679.3 36.5 %copy-start.19 = (bf16[2,512,384]{1,2,0:T(8,128)(2,1)}, bf16[2,512,384]{1,2,0:T(8,128)(2,1)S(1)}, u32[]{:S(2)}) copy-start(bf16[2,512,384]{1,2,0:T(8,128)(2,1)S(1)} %copy.132) | copy-start | bytes 2359300
  724.7 8.4 copy-start.80
  741.5 10.0 copy-start.91
  746.3 8.6 copy-start.2
  777.1 27.1 %copy-start.81 = (f32[512]{0:T(512)S(1)}, f32[512]{0:T(512)}, u32[]{:S(2)}) copy-start(f32[512]{0:T(512)} %convert_element_type.191) | copy-start | bytes 6148
  780.4 118.8 %reduce-scatter.32.cloned.1.call-start = ((), (), s32[]{:S(2)}) async-start(), calls=%async_computation.30 | async-start | bytes 1769472 | tf_op jit(solution)/shard_map/reduce_scatter | solution.py:149
  833.5 133.8 %reduce-scatter.34.cloned.1.call-start = ((), (), s32[]{:S(2)}) async-start(), calls=%async_computation.31 | async-start | bytes 1769472 | tf_op jit(solution)/shard_map/reduce_scatter | solution.py:149
  839.7 204.8 %reduce-scatter.28.cloned.1.call-start = ((), (), s32[]{:S(2)}) async-start(), calls=%async_computation.28 | async-start | bytes 3538944 | tf_op jit(solution)/shard_map/reduce_scatter | solution.py:149
  843.6 278.5 %reduce-scatter.30.cloned.1.call-start = ((), (), s32[]{:S(2)}) async-start(), calls=%async_computation.29 | async-start | bytes 3538944 | tf_op jit(solution)/shard_map/reduce_scatter | solution.py:149
  847.1 376.1 %reduce-scatter.40.cloned.1.call-start = ((), (), s32[]{:S(2)}) async-start(), calls=%async_computation.34 | async-start | bytes 811008 | tf_op jit(solution)/shard_map/reduce_scatter | solution.py:407
  850.8 473.2 %reduce-scatter.46.cloned.1.call-start = ((), (), s32[]{:S(2)}) async-start(), calls=%async_computation.37 | async-start | bytes 811008 | tf_op jit(solution)/shard_map/reduce_scatter | solution.py:410
  852.2 572.7 %reduce-scatter.48.cloned.1.call-start = ((), (), s32[]{:S(2)}) async-start(), calls=%async_computation.38 | async-start | bytes 811008 | tf_op jit(solution)/shard_map/reduce_scatter | solution.py:412
  854.5 114.9 %copy-start.52 = (bf16[2,64,512]{2,1,0:T(8,128)(2,1)S(1)}, bf16[2,64,512]{2,1,0:T(8,128)(2,1)}, u32[]{:S(2)}) copy-start(bf16[2,64,512]{2,1,0:T(8,128)(2,1)} %multiply_convert_fusion.7) | copy-start | bytes 393220
  854.5 114.9 %copy-start.67 = (bf16[2,64,1024]{2,1,0:T(8,128)(2,1)S(1)}, bf16[2,64,1024]{2,1,0:T(8,128)(2,1)}, u32[]{:S(2)}) copy-start(bf16[2,64,1024]{2,1,0:T(8,128)(2,1)} %copy-done.66) | copy-start | bytes 786436
  854.6 671.1 %reduce-scatter.50.cloned.1.call-start = ((), (), s32[]{:S(2)}) async-start(), calls=%async_computation.39 | async-start | bytes 811008 | tf_op jit(solution)/shard_map/reduce_scatter | solution.py:415
  855.9 770.6 %reduce-scatter.42.cloned.1.call-start = ((), (), s32[]{:S(2)}) async-start(), calls=%async_computation.35 | async-start | bytes 811008 | tf_op jit(solution)/shard_map/reduce_scatter | solution.py:408
  901.3 70.0 %copy-start.65 = (bf16[2,64,1024]{2,1,0:T(8,128)(2,1)S(1)}, bf16[2,64,1024]{2,1,0:T(8,128)(2,1)}, u32[]{:S(2)}) copy-start(bf16[2,64,1024]{2,1,0:T(8,128)(2,1)} %copy-done.64) | copy-start | bytes 786436
  901.3 826.2 %reduce-scatter.44.cloned.1.call-start = ((), (), s32[]{:S(2)}) async-start(), calls=%async_computation.36 | async-start | bytes 811008 | tf_op jit(solution)/shard_map/reduce_scatter | solution.py:409
  969.4 899.5 %reduce-scatter.52.cloned.1.call-start = ((), (), s32[]{:S(2)}) async-start(), calls=%async_computation.40 | async-start | bytes 2162688 | tf_op jit(solution)/shard_map/reduce_scatter | solution.py:417
  971.3 1036.0 %reduce-scatter.54.cloned.1.call-start = ((), (), s32[]{:S(2)}) async-start(), calls=%async_computation.41 | async-start | bytes 2162688 | tf_op jit(solution)/shard_map/reduce_scatter | solution.py:418
  973.3 1173.3 %reduce-scatter.56.cloned.1.call-start = ((), (), s32[]{:S(2)}) async-start(), calls=%async_computation.42 | async-start | bytes 2162688 | tf_op jit(solution)/shard_map/reduce_scatter | solution.py:419
  975.3 1269.8 %reduce-scatter.58.cloned.1.call-start = ((), (), s32[]{:S(2)}) async-start(), calls=%async_computation.43 | async-start | bytes 811008
  1045.8 78.8 %copy-start.25 = (bf16[512,512]{1,0:T(8,128)(2,1)S(1)}, bf16[512,512]{1,0:T(8,128)(2,1)}, u32[]{:S(2)}) copy-start(bf16[512,512]{1,0:T(8,128)(2,1)} %all_gather.102) | copy-start | bytes 1572868
  1047.0 1298.9 %reduce-scatter.60.cloned.1.call-start = ((), (), s32[]{:S(2)}) async-start(), calls=%async_computation.44 | async-start | bytes 811008
  1124.6 1372.1 %reduce-scatter.38.cloned.1.call-start = ((), (), s32[]{:S(2)}) async-start(), calls=%async_computation.33 | async-start | bytes 9437184 | tf_op jit(solution)/shard_map/reduce_scatter | solution.py:403
  1132.6 1514.7 %reduce-scatter.36.cloned.1.call-start = ((), (), s32[]{:S(2)}) async-start(), calls=%async_computation.32 | async-start | bytes 9437184 | tf_op jit(solution)/shard_map/reduce_scatter | solution.py:402
  1157.4 46.2 %copy-start.51 = (bf16[512,384]{1,0:T(8,128)(2,1)S(1)}, bf16[512,384]{1,0:T(8,128)(2,1)}, u32[]{:S(2)}) copy-start(bf16[512,384]{1,0:T(8,128)(2,1)} %copy-done.50) | copy-start | bytes 1179652
  1157.4 46.2 %copy-start.63 = (f32[2,128,384]{1,2,0:T(8,128)S(1)}, f32[2,128,384]{1,2,0:T(8,128)}, u32[]{:S(2)}) copy-start(f32[2,128,384]{1,2,0:T(8,128)} %reduce-scatter.28.cloned.1.call-done) | copy-start | bytes 1179652
  1157.4 46.5 %copy-start.41 = (bf16[512,384]{1,0:T(8,128)(2,1)S(1)}, bf16[512,384]{1,0:T(8,128)(2,1)}, u32[]{:S(2)}) copy-start(bf16[512,384]{1,0:T(8,128)(2,1)} %copy-done.40) | copy-start | bytes 1179652
  1157.4 46.5 %copy-start.62 = (f32[2,128,384]{1,2,0:T(8,128)S(1)}, f32[2,128,384]{1,2,0:T(8,128)}, u32[]{:S(2)}) copy-start(f32[2,128,384]{1,2,0:T(8,128)} %reduce-scatter.30.cloned.1.call-done) | copy-start | bytes 1179652
  (85 other events, 191.8 us)
Sparse Core Ops, SparseCore 0:
  10.1 79.8 all-gather.13
  92.8 44.4 all-gather.15
  155.9 42.8 all-gather.17
  201.7 23.9 reduce-scatter.23
  228.6 54.0 all-gather.19
  285.7 52.7 all-gather.21
  341.5 53.0 all-gather.23
  396.8 75.5 all-gather.25
  780.6 23.6 reduce-scatter.25
  833.6 65.5 reduce-scatter.31
  902.6 64.5 reduce-scatter.33
  970.7 73.7 reduce-scatter.27
  1048.1 73.9 reduce-scatter.29
  1127.7 95.4 reduce-scatter.39
  1228.7 95.2 reduce-scatter.45
  1329.6 95.2 reduce-scatter.47
  1430.4 95.2 reduce-scatter.49
  1531.2 95.2 reduce-scatter.41
  1632.1 95.3 reduce-scatter.43
  1730.2 138.6 reduce-scatter.51
  1871.7 135.5 reduce-scatter.53
  2010.1 136.4 reduce-scatter.55
  2152.3 92.7 reduce-scatter.57
  2250.6 95.2 reduce-scatter.59
  2350.1 146.5 reduce-scatter.37
  2500.8 146.5 reduce-scatter.35
where the time goes:
time: 2660 us
  waiting for transfers between devices  1720 us (65%)
  blocking collectives  733 us (28%)
  matrix products  78.7 us (3%)
  local copies, waits for them, and re-layouts  60.5 us (2%)
  other arithmetic  39 us (1%)
    reduce_scatter x4, waiting for transfers between devices, scatter_keys(): return lax.psum_scatter(parts, 'gy', scatter_dimension=1, tiled=True)  253 us
    unnamed x28, waiting for transfers between devices  203 us
    reduce_scatter x1, waiting for transfers between devices, per_device(): lax.psum_scatter(head_portion, 'gy', scatter_dimension=0, tiled=True)  151 us
    reduce_scatter x1, waiting for transfers between devices, per_device(): lax.psum_scatter(embed_part, 'gy', scatter_dimension=0, tiled=True)  151 us
    reduce_scatter x1, waiting for transfers between devices, per_device(): lax.psum_scatter(gate_grad, ('gx', 'gy'), scatter_dimension=0, tiled=True)  141 us
    reduce_scatter x1, waiting for transfers between devices, per_device(): lax.psum_scatter(down_grad, ('gx', 'gy'), scatter_dimension=0, tiled=True)  139 us
    reduce_scatter x1, waiting for transfers between devices, per_device(): lax.psum_scatter(up_gradient, ('gx', 'gy'), scatter_dimension=0, tiled=True)  138 us
    reduce_scatter x1, waiting for transfers between devices, per_device(): lax.psum_scatter(self_value_grad, ('gx', 'gy'), scatter_dimension=0, tile...  101 us
  transfers between devices with their start and end apart: 26, of which 18 were waited for; matrix products, arithmetic and copies ran while one was open for 4% of the time, Pallas kernels for 0%

commit v1 on v0

v1 whole, which is shorter than its diff:
```python
import functools
import math

import jax
import jax.numpy as jnp
from jax import lax
from jax.experimental import pallas as pl
from jax.experimental.pallas import tpu as pltpu
from jax.sharding import PartitionSpec as P

HEADS = 6
HEAD = 64
HD = HEADS * HEAD
BUCKETS = 32
GAIN_PAD = 128

eps = 1e-06
masked_score = -1000000000.0
bf16 = jnp.bfloat16
f32 = jnp.float32


def bits_of(axis, size):
    weights = []
    weight = size // 2
    while weight >= 1:
        weights.append((axis, weight))
        weight //= 2
    return tuple(weights)


def bit_value(bit):
    return (lax.axis_index(bit[0]) // bit[1]) % 2


def partner_of(bit):
    axis, weight = bit
    index = lax.axis_index(axis)
    return {axis: index + weight - 2 * weight * bit_value(bit)}


class Gather:
    def __init__(self, block, bits, order, halves=False):
        self.value = block
        self.bits = bits
        self.order = order
        self.halves = halves
        shape = block.shape[1:] if halves else block.shape
        self.stages = len(order)
        self.out = jax.ShapeDtypeStruct((2,) * len(bits) + shape, block.dtype)
        self.in_spec = pl.BlockSpec(memory_space=pltpu.VMEM)
        self.out_spec = pl.BlockSpec(memory_space=pl.ANY)
        self.scratch = [
            pltpu.SemaphoreType.DMA((self.stages,)),
            pltpu.SemaphoreType.DMA((self.stages,)),
            pltpu.SemaphoreType.DMA,
        ]

    def prepare(self, refs):
        self.source, self.target, self.send, self.recv, self.local_sem = refs
        self.own = [bit_value(bit) for bit in self.bits]
        self.local = pltpu.make_async_copy(
            self.source.at[self.own[self.order[0]]] if self.halves else self.source,
            self.target.at[tuple(self.own)],
            self.local_sem,
        )
        self.local.start()

    def start(self, stage):
        if stage == 1:
            self.local.wait()
        known = self.order[:stage]
        where = tuple(
            slice(None) if place in known else self.own[place] for place in range(len(self.bits))
        )
        if stage == 0:
            first = self.own[self.order[0]]
            source = self.source.at[1 - first] if self.halves else self.source
        else:
            source = self.target.at[where]
        self.copy = pltpu.make_async_remote_copy(
            src_ref=source,
            dst_ref=self.target.at[where],
            send_sem=self.send.at[stage],
            recv_sem=self.recv.at[stage],
            device_id=partner_of(self.bits[self.order[stage]]),
            device_id_type=pl.DeviceIdType.MESH,
        )
        self.copy.start()

    def finish(self, stage):
        self.copy.wait()
        if stage == self.stages - 1 and self.stages == 1:
            self.local.wait()


class Scatter:
    def __init__(self, value, bits, order, out_dtype=f32, halves=False):
        self.value = value
        self.bits = bits
        self.order = order
        self.halves = halves
        self.stages = len(order)
        count = len(bits)
        block = value.shape[count:]
        self.block = block
        self.out = jax.ShapeDtypeStruct(((2,) if halves else ()) + block, out_dtype)
        self.in_spec = pl.BlockSpec(memory_space=pltpu.VMEM)
        self.out_spec = pl.BlockSpec(memory_space=pltpu.VMEM)
        self.scratch = [
            pltpu.VMEM((2,) * (count - 1 - stage) + block, value.dtype)
            for stage in range(self.stages)
        ] + [
            pltpu.SemaphoreType.DMA((self.stages,)),
            pltpu.SemaphoreType.DMA((self.stages,)),
        ]

    def prepare(self, refs):
        self.source, self.target = refs[0], refs[1]
        self.landing = refs[2 : 2 + self.stages]
        self.send, self.recv = refs[2 + self.stages :]
        self.own = [bit_value(bit) for bit in self.bits]

    def start(self, stage):
        held = self.source if stage == 0 else self.landing[stage - 1]
        left = [place for place in range(len(self.bits)) if place not in self.order[:stage]]
        this = self.order[stage]
        where = tuple(1 - self.own[place] if place == this else slice(None) for place in left)
        self.copy = pltpu.make_async_remote_copy(
            src_ref=held.at[where],
            dst_ref=self.landing[stage],
            send_sem=self.send.at[stage],
            recv_sem=self.recv.at[stage],
            device_id=partner_of(self.bits[this]),
            device_id_type=pl.DeviceIdType.MESH,
        )
        self.copy.start()

    def finish(self, stage):
        held = self.source if stage == 0 else self.landing[stage - 1]
        landed = self.landing[stage]
        left = [place for place in range(len(self.bits)) if place not in self.order[:stage]]
        this = self.order[stage]
        last = stage == self.stages - 1
        self.copy.wait()
        rows, columns = self.block
        step = min(rows, max(16, 32768 // columns // 16 * 16))
        while rows % step:
            step -= 16
        pieces = rows // step
        free = len(left) - 1
        own = self.own[this]

        def piece(number, carry):
            place_rows = pl.ds(pl.multiple_of((number % pieces) * step, step), step)
            which = number // pieces
            inner = []
            for level in reversed(range(free)):
                inner.append((which // (2**level)) % 2)
            inner = tuple(inner)
            spot = left.index(this)
            outer = inner[:spot] + (own,) + inner[spot:]
            mine = held[outer + (place_rows,)]
            theirs = landed[inner + (place_rows,)]
            if not last:
                landed[inner + (place_rows,)] = mine + theirs
            elif self.halves:
                self.target[(own, place_rows)] = mine.astype(self.target.dtype)
                self.target[(1 - own, place_rows)] = theirs.astype(self.target.dtype)
            else:
                self.target[(place_rows,)] = (mine.astype(f32) + theirs.astype(f32)).astype(
                    self.target.dtype
                )
            return carry

        lax.fori_loop(0, pieces * 2**free, piece, 0)


def exchange(name, collective_id, jobs):
    sizes = [len(job.scratch) for job in jobs]
    bits = []
    for job in jobs:
        for bit in job.bits:
            if bit not in bits:
                bits.append(bit)

    def kernel(*refs):
        count = len(jobs)
        scratch = refs[2 * count :]
        offset = 0
        barrier = pltpu.get_barrier_semaphore()
        for bit in bits:
            pl.semaphore_signal(
                barrier, inc=1, device_id=partner_of(bit), device_id_type=pl.DeviceIdType.MESH
            )
        for place, job in enumerate(jobs):
            job.prepare(
                (refs[place], refs[count + place]) + tuple(scratch[offset : offset + sizes[place]])
            )
            offset += sizes[place]
        pl.semaphore_wait(barrier, len(bits))
        for stage in range(max(job.stages for job in jobs)):
            for job in jobs:
                if stage < job.stages:
                    job.start(stage)
            for job in jobs:
                if stage < job.stages:
                    job.finish(stage)

    outs = pl.pallas_call(
        kernel,
        name=name,
        out_shape=tuple(job.out for job in jobs),
        in_specs=[job.in_spec for job in jobs],
        out_specs=tuple(job.out_spec for job in jobs),
        scratch_shapes=[item for job in jobs for item in job.scratch],
        compiler_params=pltpu.CompilerParams(
            collective_id=collective_id, has_side_effects=True, vmem_limit_bytes=60 * 1024 * 1024
        ),
    )(*[job.value for job in jobs])
    return outs


def packed(block):
    rows, columns = block.shape
    if rows % 16 == 0:
        return block
    return block.reshape(16, rows * columns // 16)


def bucket_edges():
    edges = []
    for target in range(1, 32):
        if target < 16:
            edges.append(target)
        else:
            found = 0
            for distance in range(16, 4096):
                value = 16 + int(math.log(distance / 16.0) / math.log(8.0) * 16.0)
                if found == 0 and value >= target:
                    found = distance
            edges.append(found)
    return edges


def bucket_of(distance):
    edges = jnp.array(bucket_edges(), dtype=jnp.int32)
    return jnp.sum((distance[..., None] >= edges).astype(jnp.int32), axis=-1)


def rms_norm(rows, gain):
    return rows * lax.rsqrt(jnp.mean(rows * rows, axis=-1, keepdims=True) + eps) * gain


def gelu_tanh(value):
    return (
        0.5
        * value
        * (1.0 + jnp.tanh(0.7978845608028654 * (value + 0.044715 * value * value * value)))
    )


def norm_back(rows, gain, slope):
    _, pullback = jax.vjp(rms_norm, rows, gain)
    return pullback(slope)


def dot(left, right):
    return jnp.einsum("sd,df->sf", left, right, preferred_element_type=f32)


def dot_t(left, right):
    return jnp.einsum("sf,df->sd", left, right, preferred_element_type=f32)


def t_dot(left, right):
    return jnp.einsum("sd,sf->df", left, right, preferred_element_type=f32)


def heads_of(tensor):
    return tensor.reshape(tensor.shape[0], HEADS, HEAD)


def attend_scores(query, keys, bias, mask):
    scores = jnp.einsum("qhe,khe->hqk", heads_of(query), heads_of(keys), preferred_element_type=f32)
    if bias is not None:
        scores = jnp.where(mask[None], scores + bias, masked_score)
    return scores


def attend(query, keys, values, bias, mask):
    scores = attend_scores(query, keys, bias, mask)
    highest = jnp.max(scores, axis=-1, keepdims=True)
    log_total = highest + jnp.log(jnp.sum(jnp.exp(scores - highest), axis=-1, keepdims=True))
    shares = jnp.exp(scores - log_total).astype(bf16)
    output = jnp.einsum("hqk,khe->qhe", shares, heads_of(values), preferred_element_type=f32)
    return output.reshape(query.shape).astype(bf16), log_total


def attend_back(query, keys, values, bias, mask, log_total, out_slope):
    scores = attend_scores(query, keys, bias, mask)
    shares = jnp.exp(scores - log_total)
    out_heads = heads_of(out_slope)
    share_slope = jnp.einsum("qhe,khe->hqk", out_heads, heads_of(values), preferred_element_type=f32)
    inner = jnp.sum(shares * share_slope, axis=-1, keepdims=True)
    score_slope = (shares * (share_slope - inner)).astype(bf16)
    query_slope = jnp.einsum("hqk,khe->qhe", score_slope, heads_of(keys), preferred_element_type=f32)
    key_slope = jnp.einsum("hqk,qhe->khe", score_slope, heads_of(query), preferred_element_type=f32)
    value_slope = jnp.einsum("hqk,qhe->khe", shares.astype(bf16), out_heads, preferred_element_type=f32)
    return (
        query_slope.reshape(query.shape).astype(bf16),
        jnp.concatenate(
            [key_slope.reshape(keys.shape), value_slope.reshape(values.shape)], axis=1
        ).astype(bf16),
        score_slope,
    )


def per_device(
    target_ids,
    labels,
    lengths,
    memory,
    embedding,
    head,
    gain_self,
    w_query,
    w_key,
    w_value,
    w_out,
    relative_bias,
    gain_cross,
    c_query,
    c_key,
    c_value,
    c_out,
    gain_ff,
    w_gate,
    w_up,
    w_down,
    gain_final,
):
    micro = target_ids.shape[0]
    seq_dev = target_ids.shape[2]
    mem_dev = memory.shape[2]
    voc_dev, width = embedding.shape
    ff = w_gate.shape[1]
    n_gx = lax.axis_size("gx")
    n_gy = lax.axis_size("gy")
    column = lax.axis_index("gy")
    row_group = lax.axis_index("gx")
    seq = seq_dev * n_gy
    rows_total = micro * seq
    tok_dev = rows_total // n_gy
    per_seq = n_gy // micro
    span = n_gx * voc_dev
    own_micro = column // per_seq
    place = column % per_seq

    gx_bits = bits_of("gx", n_gx)
    gy_bits = bits_of("gy", n_gy)
    all_bits = gx_bits + gy_bits
    kx, ky = len(gx_bits), len(gy_bits)
    core = kx - 1
    outer = list(range(kx - 1))
    inner = list(range(kx, kx + ky))
    orders = (
        inner + outer + [core],
        inner[-1:] + outer + inner[:-1] + [core],
        outer + inner + [core],
    )
    gx_order = list(range(kx))
    seq_bits = gy_bits[micro.bit_length() - 1 :]
    ks = len(seq_bits)

    gains = jnp.stack([gain_self, gain_cross, gain_ff, gain_final], axis=1)
    gains = jnp.pad(gains, ((0, 0), (0, GAIN_PAD - 4)))
    shards = (
        jnp.concatenate([w_gate, w_up], axis=1),
        jnp.concatenate([w_down, c_key, c_value, c_out], axis=1),
        jnp.concatenate([w_query, w_key, w_value, w_out, c_query, gains], axis=1),
    )
    own_ids = jnp.stack([target_ids.reshape(-1), labels.reshape(-1)])
    gathered = exchange(
        "gather_weights",
        0,
        [Gather(packed(part), all_bits, order) for part, order in zip(shards, orders)]
        + [
            Gather(embedding, gx_bits, gx_order),
            Gather(head, gx_bits, gx_order),
            Gather(own_ids, gy_bits, list(range(ky))),
        ],
    )
    part_a, part_b, part_c = (
        full.reshape(n_gx * n_gy * part.shape[0], part.shape[1])
        for full, part in zip(gathered[:3], shards)
    )
    embed_rows = gathered[3].reshape(span, width)
    head_rows = gathered[4].reshape(span, width)
    ids = gathered[5].reshape(n_gy, 2, micro, seq_dev).transpose(1, 2, 0, 3).reshape(2, rows_total)

    def local_of(index):
        shard = index // voc_dev
        return jnp.where(shard % n_gy == column, shard // n_gy * voc_dev + index % voc_dev, -1)

    local_ids = local_of(ids[0])
    targets = local_of(ids[1])
    columns = jnp.arange(span, dtype=jnp.int32)
    norm_self, norm_cross, norm_ff, norm_final = (
        part_c[:, 5 * HD + number].astype(f32) for number in range(4)
    )
    qkv_w = part_c[:, : 3 * HD]
    self_query, self_kv = part_c[:, :HD], part_c[:, HD : 3 * HD]
    self_out = part_c[:, 3 * HD : 4 * HD]
    cross_query = part_c[:, 4 * HD : 5 * HD]
    down_full = part_b[:, :ff]
    cross_kv = part_b[:, ff : ff + 2 * HD]
    cross_out = part_b[:, ff + 2 * HD :]

    picked_rows = dot((local_ids[:, None] == columns[None, :]).astype(bf16), embed_rows).astype(bf16)
    memory_own = memory.reshape(micro * mem_dev, width)
    memory_kv = dot(memory_own, cross_kv).astype(bf16).reshape(micro, mem_dev, 2 * HD)
    resid0, mem_kv = exchange(
        "rows_and_memory",
        1,
        [
            Scatter(picked_rows.reshape((2,) * ky + (tok_dev, width)), gy_bits, list(range(ky))[::-1]),
            Gather(memory_kv, gy_bits, list(range(ky)), halves=True),
        ],
    )
    mem_kv = mem_kv.reshape(n_gy * mem_dev, 2 * HD)
    keys_cross, values_cross = mem_kv[:, :HD], mem_kv[:, HD:]

    live_length = lax.dynamic_index_in_dim(
        lax.dynamic_index_in_dim(lengths, own_micro, axis=0, keepdims=False), row_group, keepdims=False
    )
    query_pos = place * tok_dev + jnp.arange(tok_dev, dtype=jnp.int32)
    key_pos = jnp.arange(seq, dtype=jnp.int32)
    bucket = bucket_of(jnp.maximum(query_pos[:, None] - key_pos[None, :], 0))
    indicator = (bucket[None] == jnp.arange(BUCKETS, dtype=jnp.int32)[:, None, None]).astype(bf16)
    bias = jnp.einsum("som,ns->nom", indicator, relative_bias, preferred_element_type=f32)
    mask = (key_pos[None, :] <= query_pos[:, None]) & (key_pos[None, :] < live_length)

    normed_self = rms_norm(resid0, norm_self).astype(bf16)
    qkv = dot(normed_self, qkv_w).astype(bf16)
    query_self = qkv[:, :HD]
    (self_kv_all,) = exchange(
        "self_keys", 2, [Gather(qkv[:, HD:], seq_bits, list(range(ks))[::-1])]
    )
    self_kv_all = self_kv_all.reshape(seq, 2 * HD)
    keys_self, values_self = self_kv_all[:, :HD], self_kv_all[:, HD:]
    attn_self, total_self = attend(query_self, keys_self, values_self, bias, mask)
    resid1 = resid0 + dot_t(attn_self, self_out)
    normed_cross = rms_norm(resid1, norm_cross).astype(bf16)
    query_cross = dot(normed_cross, cross_query).astype(bf16)
    attn_cross, total_cross = attend(query_cross, keys_cross, values_cross, None, None)
    resid2 = resid1 + dot_t(attn_cross, cross_out)
    normed_ff = rms_norm(resid2, norm_ff).astype(bf16)
    gate_up = dot(normed_ff, part_a)
    gate_value, up_value = gate_up[:, :ff], gate_up[:, ff:]
    hidden = (gelu_tanh(gate_value) * up_value).astype(bf16)
    resid3 = resid2 + dot_t(hidden, down_full)
    final_rows = rms_norm(resid3, norm_final).astype(bf16)

    (states,) = exchange("final_rows", 3, [Gather(final_rows, gy_bits, list(range(ky)))])
    states = states.reshape(rows_total, width)
    logits = dot_t(states, head_rows)
    highest = jnp.max(logits, axis=1)
    spread = jnp.sum(jnp.exp(logits - highest[:, None]), axis=1)
    hit = columns[None, :] == targets[:, None]
    picked = jnp.sum(jnp.where(hit, logits, 0.0), axis=1)
    (stats,) = exchange(
        "totals", 4, [Gather(jnp.stack([highest, spread, picked]), gy_bits, list(range(ky)))]
    )
    stats = stats.reshape(n_gy, 3, rows_total)
    top = jnp.max(stats[:, 0], axis=0)
    log_total = top + jnp.log(jnp.sum(stats[:, 1] * jnp.exp(stats[:, 0] - top[None]), axis=0))
    picked = jnp.sum(stats[:, 2], axis=0)
    index = jnp.arange(rows_total, dtype=jnp.int32)
    own_lengths = lax.dynamic_index_in_dim(lengths, row_group, axis=1, keepdims=False)
    alive = (index % seq < jnp.repeat(own_lengths, seq)).astype(f32)
    loss_part = jnp.where(column == 0, jnp.sum(alive * (log_total - picked)), 0.0)
    slope = ((jnp.exp(logits - log_total[:, None]) - hit.astype(f32)) * alive[:, None]).astype(bf16)
    head_part = t_dot(slope, states).astype(bf16)
    final_part = dot(slope, head_rows).astype(bf16)
    final_slope, head_grad = exchange(
        "final_slopes",
        5,
        [
            Scatter(final_part.reshape((2,) * ky + (tok_dev, width)), gy_bits, list(range(ky))[::-1]),
            Scatter(head_part.reshape((2,) * kx + (voc_dev, width)), gx_bits, gx_order[::-1]),
        ],
    )

    grad3, norm_final_grad = norm_back(resid3, norm_final, final_slope)
    down_in = grad3.astype(bf16)
    down_grad = t_dot(down_in, hidden)
    hidden_slope = dot(down_in, down_full)
    activated, gelu_pull = jax.vjp(gelu_tanh, gate_value)
    up_slope = (hidden_slope * activated).astype(bf16)
    gate_slope = gelu_pull(hidden_slope * up_value)[0].astype(bf16)
    gate_up_slope = jnp.concatenate([gate_slope, up_slope], axis=1)
    gate_up_grad = t_dot(normed_ff, gate_up_slope)
    back_part, norm_ff_grad = norm_back(resid2, norm_ff, dot_t(gate_up_slope, part_a))
    grad2 = grad3 + back_part
    cross_in = grad2.astype(bf16)
    cross_out_grad = t_dot(cross_in, attn_cross)
    attn_slope = dot(cross_in, cross_out).astype(bf16)
    cross_query_slope, cross_kv_slope, _ = attend_back(
        query_cross, keys_cross, values_cross, None, None, total_cross, attn_slope
    )
    cross_query_grad = t_dot(normed_cross, cross_query_slope)
    back_part, norm_cross_grad = norm_back(
        resid1, norm_cross, dot_t(cross_query_slope, cross_query)
    )
    grad1 = grad2 + back_part
    self_in = grad1.astype(bf16)
    self_out_grad = t_dot(self_in, attn_self)
    attn_slope = dot(self_in, self_out).astype(bf16)
    query_slope, kv_slope, score_slope = attend_back(
        query_self, keys_self, values_self, bias, mask, total_self, attn_slope
    )
    bias_grad = jnp.einsum("noj,soj->ns", score_slope, indicator, preferred_element_type=f32)
    kv_slope, mem_slope = exchange(
        "key_slopes",
        6,
        [
            Scatter(
                kv_slope.reshape((2,) * ks + (tok_dev, 2 * HD)), seq_bits, list(range(ks)), bf16
            ),
            Scatter(
                cross_kv_slope.reshape((2,) * ky + (mem_dev, 2 * HD)),
                gy_bits,
                list(range(ky))[::-1],
                bf16,
                halves=True,
            ),
        ],
    )
    mem_slope = mem_slope.reshape(micro * mem_dev, 2 * HD)
    cross_kv_grad = t_dot(memory_own, mem_slope)
    memory_grad = dot_t(mem_slope, cross_kv)
    qkv_slope = jnp.concatenate([query_slope, kv_slope], axis=1)
    qkv_grad = t_dot(normed_self, qkv_slope)
    back_part, norm_self_grad = norm_back(resid0, norm_self, dot_t(qkv_slope, qkv_w))
    grad0 = grad1 + back_part
    (slopes,) = exchange(
        "row_slopes", 7, [Gather(grad0.astype(bf16), gy_bits, list(range(ky)))]
    )
    embed_part = t_dot(
        (local_ids[:, None] == columns[None, :]).astype(bf16), slopes.reshape(rows_total, width)
    ).astype(bf16)
    gain_grads = jnp.stack([norm_self_grad, norm_cross_grad, norm_ff_grad, norm_final_grad], axis=1)
    gain_grads = jnp.pad(gain_grads, ((0, 0), (0, GAIN_PAD - 4)))
    sums = (
        gate_up_grad.astype(bf16),
        jnp.concatenate([down_grad, cross_kv_grad, cross_out_grad], axis=1).astype(bf16),
        jnp.concatenate([qkv_grad, self_out_grad, cross_query_grad, gain_grads], axis=1).astype(bf16),
    )
    small = jnp.concatenate([bias_grad.reshape(-1), loss_part[None]])
    small = jnp.pad(small, (0, 1024 - small.shape[0])).reshape(8, 128)
    blocks = [
        part.reshape((2,) * (kx + ky) + packed_shape(part, n_gx * n_gy)) for part in sums
    ]
    grad_a, grad_b, grad_c, embedding_grad, small = exchange(
        "scatter_weights",
        8,
        [Scatter(part, all_bits, order[::-1]) for part, order in zip(blocks, orders)]
        + [
            Scatter(embed_part.reshape((2,) * kx + (voc_dev, width)), gx_bits, gx_order[::-1]),
            Gather(small, all_bits, orders[0]),
        ],
    )
    rows_dev = width // (n_gx * n_gy)
    grad_a, grad_b, grad_c = (
        grad.reshape(rows_dev, part.shape[1]) for grad, part in zip((grad_a, grad_b, grad_c), sums)
    )
    small = jnp.sum(small.reshape(n_gx * n_gy, 1024), axis=0)
    loss = small[HEADS * BUCKETS] / jnp.sum(lengths).astype(f32)
    bias_total = small[: HEADS * BUCKETS].reshape(HEADS, BUCKETS)
    gain_out = [grad_c[:, 5 * HD + number] for number in range(4)]
    return (
        loss,
        memory_grad.reshape(micro, 1, mem_dev, width),
        embedding_grad,
        head_grad,
        gain_out[0],
        grad_c[:, :HD],
        grad_c[:, HD : 2 * HD],
        grad_c[:, 2 * HD : 3 * HD],
        grad_c[:, 3 * HD : 4 * HD],
        bias_total,
        gain_out[1],
        grad_c[:, 4 * HD : 5 * HD],
        grad_b[:, ff : ff + HD],
        grad_b[:, ff + HD : ff + 2 * HD],
        grad_b[:, ff + 2 * HD :],
        gain_out[2],
        grad_a[:, :ff],
        grad_a[:, ff:],
        grad_b[:, :ff],
        gain_out[3],
    )


def packed_shape(part, count):
    rows, columns = part.shape[0] // count, part.shape[1]
    if rows % 16 == 0:
        return (rows, columns)
    return (16, rows * columns // 16)


def solution(mesh):
    placed = (
        P(None, "gx", "gy"),
        P(None, "gx", "gy"),
        P(),
        P(None, "gx", "gy", None),
        P(("gx", "gy"), None),
        P(("gx", "gy"), None),
        P(("gx", "gy")),
        P(("gx", "gy"), None),
        P(("gx", "gy"), None),
        P(("gx", "gy"), None),
        P(("gx", "gy"), None),
        P(),
        P(("gx", "gy")),
        P(("gx", "gy"), None),
        P(("gx", "gy"), None),
        P(("gx", "gy"), None),
        P(("gx", "gy"), None),
        P(("gx", "gy")),
        P(("gx", "gy"), None),
        P(("gx", "gy"), None),
        P(("gx", "gy"), None),
        P(("gx", "gy")),
    )
    return jax.shard_map(
        per_device,
        mesh=mesh,
        in_specs=placed,
        out_specs=(
            P(),
            P(None, "gx", "gy", None),
            P(("gx", "gy"), None),
            P(("gx", "gy"), None),
            P(("gx", "gy")),
            P(("gx", "gy"), None),
            P(("gx", "gy"), None),
            P(("gx", "gy"), None),
            P(("gx", "gy"), None),
            P(),
            P(("gx", "gy")),
            P(("gx", "gy"), None),
            P(("gx", "gy"), None),
            P(("gx", "gy"), None),
            P(("gx", "gy"), None),
            P(("gx", "gy")),
            P(("gx", "gy"), None),
            P(("gx", "gy"), None),
            P(("gx", "gy"), None),
            P(("gx", "gy")),
        ),
        check_vma=False,
    )
```

time: 2660 us -> 503 us (0.19)
  waiting for transfers between devices: 1720 us -> 0 us
  blocking collectives: 733 us -> 0 us
  Pallas kernels: 0 us -> 330 us
    reduce_scatter x17 -> x0, waiting for transfers between devices: 1520 us -> none  [the longest x4 253 us: scatter_keys(): return lax.psum_scatter(parts, 'gy', scatter_dimension=1, tiled=True)]
    all_gather x16 -> x0, blocking collectives: 657 us -> none  [the longest x1 76.7 us: per_device(): lax.all_gather(c_value, ('gx', 'gy'), axis=0, tiled=True)]
    pallas_call x0 -> x9, Pallas kernels: none -> 330 us  [exchange(): pl.pallas_call(kernel, name=name, out_shape=tuple((job.out for job in job...]
    unnamed x28 -> x0, waiting for transfers between devices: 203 us -> none
    psum x1 -> x0, blocking collectives: 39.5 us -> none  [per_device(): bias_total, loss_total = lax.psum((bias_gradient, loss_part), ('gx', 'gy'))]
    unnamed x1 -> x0, blocking collectives: 36.9 us -> none
    dot_general x50 -> x40, matrix products: 78.7 us -> 66.4 us  [the longest x9 19.1 us: t_dot(): return jnp.einsum('sd,sf->df', left, right, preferred_element_type=f32)]
  transfers between devices with their start and end apart: 26 -> 0, of which waited for: 18 -> 0; matrix products, arithmetic and copies ran while one was open for 4% -> 0% of each run, Pallas kernels for 0% -> 0%
where the time goes in v1:
time: 503 us; the launch traced here: 496 us
  Pallas kernels  330 us (66%)
  matrix products  66.4 us (13%)
  local copies, waits for them, and re-layouts  54.2 us (11%)
  other arithmetic  40 us (8%)
  between operations  5.31 us (1%)
    pallas_call x9, Pallas kernels, exchange(): pl.pallas_call(kernel, name=name, out_shape=tuple((job.out for job in job...  330 us
    dot_general x9, matrix products, t_dot(): return jnp.einsum('sd,sf->df', left, right, preferred_element_type=f32)  19.1 us
    dot_general x9, matrix products, dot(): return jnp.einsum('sd,df->sf', left, right, preferred_element_type=f32)  18.3 us
    unnamed x158, local copies, waits for them, and re-layouts  14.6 us
    dot_general x8, matrix products, dot_t(): return jnp.einsum('sf,df->sd', left, right, preferred_element_type=f32)  13.4 us
    concatenate x8, local copies, waits for them, and re-layouts, attend_back(): jnp.concatenate([key_slope.reshape(keys.shape), value_slope.reshape(value...  11.5 us

profile of v1, /device:TPU:0, one launch (start us, length us, event | category | flops | bytes accessed | tf_op | source)
XLA Modules:
  0.0 495.6 jit_solution(10751907653230837357)
XLA Ops:
  0.7 1.3 dynamic_slice.10
  2.0 1.3 reduce_sum.290
  6.0 1.3 reduce.24
  7.5 1.3 reduce.23
  15.3 1.4 pad_maximum_fusion.11.refs_0_
  16.7 1.4 pad_maximum_fusion.10.refs_1_
  18.3 1.5 convert_reduce_fusion
  19.9 2.0 fusion.1
  22.0 1.7 copy.146
  23.7 71.7 %gather_weights.1 = (bf16[2,2,2,2,2,16,2048]{6,5,4,3,2,1,0:T(8,128)(2,1)}, bf16[2,2,2,2,2,16,2176]{6,5,4,3,2,1,0:T(8,128)(2,1)}, bf16[2,2,2,2,2,16,2048]{6,5,4,3...) custom-call(bf16[16,2048]{1,0:T(8,128)(2,1)} %pad_maximum_fusion.11., ...), custom_call_target="tpu_custom_call" | custom-call | tf_op jit(solution)/shard_map/gather_weights/pallas_call | solution.py:210
  96.4 4.9 fusion.11
  101.3 2.2 convolution_convert_fusion.9
  103.6 50.5 %rows_and_memory.1 = (f32[128,512]{1,0:T(8,128)}, bf16[2,2,2,128,768]{4,3,2,1,0:T(8,128)(2,1)}) custom-call(bf16[2,2,2,128,512]{4,3,2,1,0:T(8,128)(2,1)} %bitcast.219, bf16[2,128,768]{2,1,0:T(8,128)(2,1)} %bitcast.240), custom_call_target="tpu_custom_call" | custom-call | tf_op jit(solution)/shard_map/rows_and_memory/pallas_call | solution.py:210
  154.1 1.6 fusion.93
  155.6 1.2 copy.150
  157.0 1.2 copy.147
  158.2 2.1 slice_convert_fusion
  162.9 14.7 %self_keys.1 = bf16[2,2,128,768]{3,2,1,0:T(8,128)(2,1)} custom-call(bf16[128,768]{1,0:T(8,128)(2,1)} %slice.173.refs_0_), custom_call_target="tpu_custom_call" | custom-call | tf_op jit(solution)/shard_map/self_keys/pallas_call | solution.py:210
  177.6 1.9 fusion.94
  180.5 1.5 fusion.99
  182.6 1.3 copy.142
  184.4 1.4 multiply_reduce_fusion.12
  186.5 1.3 convolution_convert_fusion.21
  187.9 1.9 fusion.100
  196.0 22.2 %final_rows.1 = bf16[2,2,2,128,512]{4,3,2,1,0:T(8,128)(2,1)} custom-call(bf16[128,512]{1,0:T(8,128)(2,1)} %multiply_convert_fusion.5.refs_0_), custom_call_target="tpu_custom_call" | custom-call | tf_op jit(solution)/shard_map/final_rows/pallas_call | solution.py:210
  218.2 4.4 fusion.101
  222.6 2.6 exponential_reduce_fusion
  226.4 13.0 %totals.1 = f32[2,2,2,3,1024]{4,3,2,1,0:T(4,128)} custom-call(f32[3,1024]{1,0:T(4,128)} %pad_maximum_fusion.12.refs_0_), custom_call_target="tpu_custom_call" | custom-call | tf_op jit(solution)/shard_map/totals/pallas_call | solution.py:210
  242.0 5.4 %multiply_convert_fusion = bf16[1024,2048]{1,0:T(8,128)(2,1)S(1)} fusion(f32[1024,2048]{1,0:T(8,128)} %copy-done.3, f32[1024]{0:T(1024)S(1)} %fusion.77, f32[1024]{0:T(1024)S(1)} %get-tuple-element.151, s32[1024]{0:T(1024)S(1)} %get-tuple-element.201), kind=kLoop, calls=%fused_computation | loop fusion | flops 12582912 | bytes 12595200 | tf_op jit(solution)/shard_map/convert_element_type | solution.py:483
  247.4 3.3 convolution_convert_fusion.5
  250.7 3.8 convolution_convert_fusion.1
  254.4 33.9 %final_slopes.1 = (f32[128,512]{1,0:T(8,128)}, f32[512,512]{1,0:T(8,128)}) custom-call(bf16[2,2,2,128,512]{4,3,2,1,0:T(8,128)(2,1)} %bitcast.215, bf16[2,2,512,512]{3,2,1,0:T(8,128)(2,1)} %bitcast.209), custom_call_target="tpu_custom_call" | custom-call | tf_op jit(solution)/shard_map/final_slopes/pallas_call | solution.py:210
  290.6 2.3 fusion.30
  295.1 1.5 convert_bitcast_fusion.1
  297.3 1.9 convolution_convert_fusion.19
  300.3 2.0 convolution_convert_fusion.12
  302.3 2.5 convolution_convert_fusion.4
  304.7 1.6 fusion.13
  306.3 3.2 concatenate.63
  309.6 3.2 copy.159
  312.9 3.3 convolution_convert_fusion
  320.9 1.3 pad_maximum_fusion.2.refs_1_
  322.2 1.4 multiply_reduce_fusion.5
  323.9 1.4 convolution_convert_fusion.17
  326.8 1.2 fusion.15
  329.1 1.3 copy.157
  332.9 1.3 copy.156
  334.2 2.0 pad_maximum_fusion.3.refs_0_
  336.2 36.4 %key_slopes.1 = (bf16[128,768]{1,0:T(8,128)(2,1)}, bf16[2,128,768]{2,1,0:T(8,128)(2,1)}) custom-call(bf16[2,2,128,768]{3,2,1,0:T(8,128)(2,1)} %pad_maximum_fusion.3.refs_0_, bf16[2,2,2,128,768]{4,3,2,1,0:T(8,128)(2,1)} %pad_maximum_fusion.2.refs_1_), custom_call_target="tpu_custom_call" | custom-call | tf_op jit(solution)/shard_map/key_slopes/pallas_call | solution.py:210
  372.7 2.0 multiply_reduce_fusion.2
  374.8 2.4 convolution_bitcast_fusion
  378.2 1.7 copy.168
  379.9 3.0 fusion.17
  384.2 1.6 pad_maximum_fusion.refs_1_
  386.3 1.6 pad_maximum_fusion.1.refs_2_
  388.0 22.0 %row_slopes.1 = bf16[2,2,2,128,512]{4,3,2,1,0:T(8,128)(2,1)} custom-call(bf16[128,512]{1,0:T(8,128)(2,1)} %fusion.46.refs_0_), custom_call_target="tpu_custom_call" | custom-call | tf_op jit(solution)/shard_map/row_slopes/pallas_call | solution.py:210
  409.9 5.4 %fusion.8 = bf16[2048,512]{1,0:T(8,128)(2,1)} fusion(bf16[1024,512]{1,0:T(8,128)(2,1)} %bitcast.218, s32[1024]{0:T(1024)S(1)} %copy-done.63), kind=kOutput, calls=%fused_computation.21 | convolution fusion | flops 2150629376 | bytes 3149824 | tf_op jit(solution)/shard_map/sd,sf->df/dot_general | solution.py:277
  415.3 65.3 %scatter_weights.1 = (f32[16,2048]{1,0:T(8,128)}, f32[16,2176]{1,0:T(8,128)}, f32[16,2048]{1,0:T(8,128)}, f32[512,512]{1,0:T(8,128)}, f32[2,2,2,2,2,8,128]{6,5,4,3,2,1,0:T(8,128)}) custom-call(bf16[2,2,2,2,2,16,2048]{6,5,4,3,2,1,0:T(8,128)(2,1)} %bitcast.183, bf16[2,2,2,2,2,16,2176]{6,5,4,3,2,1,0:T(8,128)(2,1)} %pad_maximum_fusion.refs_1_, ...), custom_call_target="tpu_custom_call" | custom-call | tf_op jit(solution)/shard_map/scatter_weights/pallas_call | solution.py:210
  482.9 1.6 slice_reduce_fusion.1
  484.5 1.5 fusion.97
  486.6 1.5 slice.167
  488.1 1.4 fusion.95
  489.5 1.5 fusion.96
  491.0 2.3 copy.209
  (246 shorter events, 46.6 us)
Async XLA Ops:
  0.7 4.9 copy-start
  15.3 8.4 %copy-start.52 = (bf16[16,2048]{1,0:T(8,128)(2,1)}, bf16[16,2048]{1,0:T(8,128)(2,1)S(1)}, u32[]{:S(2)}) copy-start(bf16[16,2048]{1,0:T(8,128)(2,1)S(1)} %constant_dynamic-update-slice_fusion.refs_2_) | copy-start | bytes 196612
  19.9 3.7 copy-start.38
  96.4 5.0 copy-start.62
  154.1 2.8 copy-start.15
  156.9 4.6 copy-start.68
  157.0 4.7 copy-start.64
  157.0 4.7 copy-start.28
  161.7 17.9 %copy-start.53 = (f32[512,1]{0,1:T(1,128)}, f32[512,1]{0,1:T(1,128)S(1)}, u32[]{:S(2)}) copy-start(f32[512,1]{0,1:T(1,128)S(1)} %copy.186) | copy-start | bytes 6148
  162.1 18.4 %copy-start.12 = (f32[128,512,6]{1,0,2:T(8,128)S(1)}, f32[128,512,6]{1,0,2:T(8,128)}, u32[]{:S(2)}) copy-start(f32[128,512,6]{1,0,2:T(8,128)} %copy.146) | copy-start | bytes 4718596
  162.9 19.1 %copy-start.45 = (bf16[128,384]{0,1:T(8,128)(2,1)}, bf16[128,384]{0,1:T(8,128)(2,1)S(1)}, u32[]{:S(2)}) copy-start(bf16[128,384]{0,1:T(8,128)(2,1)S(1)} %copy.143) | copy-start | bytes 294916
  182.0 2.3 copy-start.1
  182.0 2.3 copy-start.16
  183.8 4.0 copy-start.20
  184.3 3.5 copy-start.40
  185.8 4.0 copy-start.66
  186.5 1.4 copy-start.58
  187.9 2.8 copy-start.42
  189.8 1.1 copy-start.5
  190.6 1.0 copy-start.8
  190.7 1.8 copy-start.24
  190.9 2.2 copy-start.29
  191.7 1.9 copy-start.44
  193.1 99.9 %copy-start.60 = (f32[128]{0:T(128)}, f32[128]{0:T(128)S(1)}, u32[]{:S(2)}) copy-start(f32[128]{0:T(128)S(1)} %fusion.83) | copy-start | bytes 1540
  222.6 3.2 copy-start.3
  222.6 18.1 %copy-start.55 = (s32[1,4,2,128]{3,1,2,0:T(4,128)S(1)}, s32[1,4,2,128]{3,1,2,0:T(4,128)}, u32[]{:S(2)}) copy-start(s32[1,4,2,128]{3,1,2,0:T(4,128)} %copy.185) | copy-start | bytes 12292
  241.9 5.4 %copy-start.70 = (bf16[2,2,512,512]{3,2,1,0:T(8,128)(2,1)S(1)}, bf16[2,2,512,512]{3,2,1,0:T(8,128)(2,1)}, u32[]{:S(2)}) copy-start(bf16[2,2,512,512]{3,2,1,0:T(8,128)(2,1)} %get-tuple-element.44) | copy-start | bytes 6291460
  247.3 3.3 copy-start.36
  254.4 34.0 %copy-start.19 = (f32[128,512]{1,0:T(8,128)S(1)}, f32[128,512]{1,0:T(8,128)}, u32[]{:S(2)}) copy-start(f32[128,512]{1,0:T(8,128)} %copy-done.18) | copy-start | bytes 786436
  290.5 4.6 copy-start.27
  290.6 2.4 copy-start.11
  290.6 2.4 copy-start.30
  292.9 3.7 copy-start.49
  292.9 3.6 copy-start.50
  306.3 6.5 %copy-start.61 = (f32[128]{0:T(128)S(1)}, f32[128]{0:T(128)}, u32[]{:S(2)}) copy-start(f32[128]{0:T(128)} %copy-done.60) | copy-start | bytes 1540
  312.8 3.3 copy-start.6
  317.1 1.1 copy-start.4
  319.5 1.3 copy-start.23
  320.1 2.1 copy-start.9
  320.1 2.1 copy-start.59
  320.9 2.7 copy-start.67
  320.9 2.7 copy-start.26
  322.2 3.6 copy-start.41
  323.6 3.3 copy-start.2
  325.8 4.6 copy-start.21
  331.0 1.5 copy-start.46
  332.0 2.2 copy-start.33
  332.5 40.1 %copy-start.47 = (bf16[128,384]{1,0:T(8,128)(2,1)}, bf16[128,384]{1,0:T(8,128)(2,1)S(1)}, u32[]{:S(2)}) copy-start(bf16[128,384]{1,0:T(8,128)(2,1)S(1)} %copy.162) | copy-start | bytes 294916
  334.2 38.5 %copy-start.17 = (f32[128,512]{1,0:T(8,128)S(1)}, f32[128,512]{1,0:T(8,128)}, u32[]{:S(2)}) copy-start(f32[128,512]{1,0:T(8,128)} %get-tuple-element.40) | copy-start | bytes 786436
  334.2 38.5 %copy-start.54 = (f32[512,1]{0,1:T(1,128)S(1)}, f32[512,1]{0,1:T(1,128)}, u32[]{:S(2)}) copy-start(f32[512,1]{0,1:T(1,128)} %copy-done.53) | copy-start | bytes 6148
  334.2 38.5 %copy-start.65 = (f32[128]{0:T(128)S(1)}, f32[128]{0:T(128)}, u32[]{:S(2)}) copy-start(f32[128]{0:T(128)} %copy-done.64) | copy-start | bytes 1540
  372.6 2.1 copy-start.34
  372.7 4.5 copy-start.69
  372.7 5.3 %copy-start.56 = (bf16[512,1]{0,1:T(2,128)(2,1)S(1)}, bf16[512,1]{0,1:T(2,128)(2,1)}, u32[]{:S(2)}) copy-start(bf16[512,1]{0,1:T(2,128)(2,1)} %stack.62) | copy-start | bytes 3076
  372.7 5.3 %copy-start.57 = (bf16[512,1]{0,1:T(2,128)(2,1)S(1)}, bf16[512,1]{0,1:T(2,128)(2,1)}, u32[]{:S(2)}) copy-start(bf16[512,1]{0,1:T(2,128)(2,1)} %stack.63) | copy-start | bytes 3076
  374.8 5.1 %copy-start.39 = (s32[128,512]{0,1:T(8,128)S(1)}, s32[128,512]{0,1:T(8,128)}, u32[]{:S(2)}) copy-start(s32[128,512]{0,1:T(8,128)} %copy-done.38) | copy-start | bytes 786436
  379.9 3.8 copy-start.35
  379.9 4.2 copy-start.14
  379.9 4.2 copy-start.31
  384.1 1.6 copy-start.48
  384.2 1.6 copy-start.51
  384.2 2.2 copy-start.32
  386.3 23.6 %copy-start.63 = (s32[1024]{0:T(1024)S(1)}, s32[1024]{0:T(1024)}, u32[]{:S(2)}) copy-start(s32[1024]{0:T(1024)} %copy-done.62) | copy-start | bytes 12292
  480.6 12.6 %copy-start.37 = (f32[512,512]{1,0:T(8,128)S(1)}, f32[512,512]{1,0:T(8,128)}, u32[]{:S(2)}) copy-start(f32[512,512]{1,0:T(8,128)} %get-tuple-element.225) | copy-start | bytes 3145732
  (7 other events, 6.1 us)

commit v2 on v1

v2 whole, which is shorter than its diff:
```python
import functools
import itertools
import math

import jax
import jax.numpy as jnp
from jax import lax
from jax.experimental import pallas as pl
from jax.experimental.pallas import tpu as pltpu
from jax.sharding import PartitionSpec as P

HEADS = 6
HEAD = 64
HD = HEADS * HEAD
BUCKETS = 32
GAIN_PAD = 128

eps = 1e-06
masked_score = -1000000000.0
bf16 = jnp.bfloat16
f32 = jnp.float32


def flip(position, offset):
    moved = position
    weight = 1
    while weight <= offset:
        if offset & weight:
            moved = moved + weight * (1 - 2 * ((position // weight) % 2))
        weight *= 2
    return moved


def coordinates():
    gx, gy = lax.axis_index("gx"), lax.axis_index("gy")
    return {"a": gx // 2, "c": gx % 2, "s": gy // 2, "h": gy % 2}


def peer_of(dim, offset):
    gx, gy = lax.axis_index("gx"), lax.axis_index("gy")
    if dim == "a":
        return {"gx": 2 * flip(gx // 2, offset) + gx % 2}
    if dim == "c":
        return {"gx": flip(gx, 1)}
    if dim == "s":
        return {"gy": 2 * flip(gy // 2, offset) + gy % 2}
    return {"gy": flip(gy, 1)}


def remote(source, target, send, recv, dim, offset):
    return pltpu.make_async_remote_copy(
        src_ref=source,
        dst_ref=target,
        send_sem=send,
        recv_sem=recv,
        device_id=peer_of(dim, offset),
        device_id_type=pl.DeviceIdType.MESH,
    )


def each_piece(rows, columns, body, width=16384):
    step = rows
    while step * columns > width and step % 32 == 0:
        step //= 2
    if step == rows:
        body(slice(None))
        return

    def piece(number, carry):
        body(pl.ds(pl.multiple_of(number * step, step), step))
        return carry

    lax.fori_loop(0, rows // step, piece, 0)


class Gather:
    def __init__(self, block, order, layout, sizes, merged=""):
        self.value = block
        self.order, self.layout, self.sizes, self.merged = order, layout, sizes, merged
        self.out = jax.ShapeDtypeStruct(tuple(sizes[d] for d in layout) + block.shape, block.dtype)
        self.in_spec = pl.BlockSpec(memory_space=pltpu.VMEM)
        self.out_spec = pl.BlockSpec(memory_space=pl.ANY)
        self.transfers = []
        for level, dim in enumerate(order):
            ranges = [(None,) if d in merged else range(sizes[d]) for d in order[:level]]
            for unit in itertools.product(*ranges):
                for offset in range(1, sizes[dim]):
                    self.transfers.append((level, unit, offset))
        self.index = {transfer: number for number, transfer in enumerate(self.transfers)}
        count = len(self.transfers)
        self.scratch = [
            pltpu.SemaphoreType.DMA((count,)),
            pltpu.SemaphoreType.DMA((count,)),
            pltpu.SemaphoreType.DMA,
        ]
        self.peers = [(d, offset) for d in order for offset in range(1, sizes[d])]

    def prepare(self, refs, place):
        self.source, self.target, self.send, self.recv, self.local_sem = refs
        self.place = place
        self.local = pltpu.make_async_copy(
            self.source, self.target.at[tuple(place[d] for d in self.layout)], self.local_sem
        )
        self.local.start()
        self.local_done = False
        self.arrived = set()
        self.sent = []

    def region(self, level, unit, offset):
        where = dict(self.place)
        for d, moved in zip(self.order[:level], unit):
            where[d] = slice(None) if moved is None else flip(self.place[d], moved)
        if offset:
            where[self.order[level]] = flip(self.place[self.order[level]], offset)
        return self.target.at[tuple(where[d] for d in self.layout)]

    def needs(self, level, unit):
        if level == 0:
            return []
        last, before = unit[-1], unit[:-1]
        if last is None:
            dim = self.order[level - 1]
            return self.needs(level - 1, before) + [
                (level - 1, before, offset) for offset in range(1, self.sizes[dim])
            ]
        if last == 0:
            return self.needs(level - 1, before)
        return [(level - 1, before, last)]

    def arrive(self, transfer):
        if transfer in self.arrived:
            return
        self.arrived.add(transfer)
        level, unit, offset = transfer
        number = self.index[transfer]
        there = self.region(level, unit, offset)
        remote(
            there, there, self.send.at[number], self.recv.at[number], self.order[level], offset
        ).wait_recv()

    def launch(self, transfer):
        level, unit, offset = transfer
        number = self.index[transfer]
        for need in self.needs(level, unit):
            self.arrive(need)
        target = self.region(level, unit, 0)
        own = all(moved == 0 for moved in unit)
        if None in unit and not self.local_done:
            self.local.wait()
            self.local_done = True
        copy = remote(
            self.source if own else target,
            target,
            self.send.at[number],
            self.recv.at[number],
            self.order[level],
            offset,
        )
        copy.start()
        self.sent.append(copy)

    def events(self):
        found = []
        for transfer in self.transfers:
            level, unit, offset = transfer
            key = 0.1 * level + 0.01 * offset
            for d, moved in zip(self.order, unit):
                key += self.sizes[d] - 1 if moved is None else moved
            found.append((key, functools.partial(self.launch, transfer)))
        return found

    def finish(self):
        if not self.local_done:
            self.local.wait()
        for transfer in self.transfers:
            self.arrive(transfer)
        for copy in self.sent:
            copy.wait_send()


class Scatter:
    def __init__(self, value, order, layout, sizes, merged="", out_dtype=f32):
        self.value = value
        self.order, self.layout, self.sizes, self.merged = order, layout, sizes, merged
        self.block = value.shape[len(layout) :]
        self.out = jax.ShapeDtypeStruct(self.block, out_dtype)
        self.in_spec = pl.BlockSpec(memory_space=pltpu.VMEM)
        self.out_spec = pl.BlockSpec(memory_space=pltpu.VMEM)
        self.levels = len(order)
        self.units = []
        self.scratch = []
        self.layouts = [layout]
        for level, dim in enumerate(order):
            later = order[level + 1 :]
            ranges = [(None,) if d in merged else range(sizes[d]) for d in later]
            units = sorted(
                itertools.product(*ranges), key=lambda unit: -sum(moved or 0 for moved in unit)
            )
            self.units.append(units)
            left = "".join(d for d in self.layouts[-1] if d != dim)
            self.layouts.append(left)
            self.scratch.append(
                pltpu.VMEM(
                    (sizes[dim] - 1,) + tuple(sizes[d] for d in left) + self.block, value.dtype
                )
            )
        self.index = {}
        for level, dim in enumerate(order):
            for unit in self.units[level]:
                for offset in range(1, sizes[dim]):
                    self.index[(level, unit, offset)] = len(self.index)
        count = len(self.index)
        self.scratch += [pltpu.SemaphoreType.DMA((count,)), pltpu.SemaphoreType.DMA((count,))]
        self.peers = [(d, offset) for d in order for offset in range(1, sizes[d])]

    def prepare(self, refs, place):
        self.source, self.target = refs[0], refs[1]
        self.landing = refs[2 : 2 + self.levels]
        self.send, self.recv = refs[2 + self.levels :]
        self.place = place
        self.sent = []

    def held(self, level):
        return self.source if level == 0 else self.landing[level - 1].at[0]

    def later(self, level, unit):
        where = {}
        for d, moved in zip(self.order[level + 1 :], unit):
            where[d] = slice(None) if moved is None else flip(self.place[d], moved)
        return where

    def copy(self, level, unit, offset):
        number = self.index[(level, unit, offset)]
        dim = self.order[level]
        where = self.later(level, unit)
        landed = self.landing[level].at[
            (offset - 1,) + tuple(where[d] for d in self.layouts[level + 1])
        ]
        where[dim] = flip(self.place[dim], offset)
        source = self.held(level).at[tuple(where[d] for d in self.layouts[level])]
        return remote(source, landed, self.send.at[number], self.recv.at[number], dim, offset)

    def launch(self, level, unit, offset):
        copy = self.copy(level, unit, offset)
        copy.start()
        self.sent.append(copy)

    def reduce(self, level, unit):
        dim = self.order[level]
        size = self.sizes[dim]
        for offset in range(1, size):
            self.copy(level, unit, offset).wait_recv()
        where = self.later(level, unit)
        free = [d for d in self.order[level + 1 :] if isinstance(where[d], slice)]
        total = math.prod(self.sizes[d] for d in free)
        rows, columns = self.block
        last = level == self.levels - 1

        def one(number, carry):
            at = dict(where)
            rest = number
            for d in free:
                at[d] = rest % self.sizes[d]
                rest = rest // self.sizes[d]
            spot = tuple(at[d] for d in self.layouts[level + 1])
            at[dim] = self.place[dim]
            mine = tuple(at[d] for d in self.layouts[level])

            def body(piece):
                result = self.held(level)[mine + (piece,)].astype(f32)
                for offset in range(1, size):
                    result = result + self.landing[level][(offset - 1,) + spot + (piece,)].astype(f32)
                if last:
                    self.target[(piece,)] = result.astype(self.target.dtype)
                else:
                    self.landing[level][(0,) + spot + (piece,)] = result.astype(self.landing[level].dtype)

            each_piece(rows, columns, body)
            return carry

        if total == 1:
            one(0, 0)
        else:
            lax.fori_loop(0, total, one, 0)
        if not last:
            ahead, rest = unit[0], unit[1:]
            if ahead is None:
                offsets = range(1, self.sizes[self.order[level + 1]])
            else:
                offsets = [ahead] if ahead else []
            for offset in offsets:
                self.launch(level + 1, rest, offset)

    def events(self):
        found = []
        for number, unit in enumerate(self.units[0]):
            for offset in range(1, self.sizes[self.order[0]]):
                found.append(
                    (-1 + 0.001 * number, functools.partial(self.launch, 0, unit, offset))
                )
        for level in range(self.levels):
            count = len(self.units[level])
            for number, unit in enumerate(self.units[level]):
                found.append(
                    (level + number / count, functools.partial(self.reduce, level, unit))
                )
        return found

    def finish(self):
        for copy in self.sent:
            copy.wait_send()


class MemoryGather:
    def __init__(self, memory, sizes):
        self.value = memory
        self.sizes = sizes
        self.out = jax.ShapeDtypeStruct((sizes["s"], 2) + memory.shape[1:], memory.dtype)
        self.in_spec = pl.BlockSpec(memory_space=pltpu.VMEM)
        self.out_spec = pl.BlockSpec(memory_space=pl.ANY)
        rows = sizes["s"]
        self.scratch = [
            pltpu.SemaphoreType.DMA((2, rows)),
            pltpu.SemaphoreType.DMA((2, rows)),
            pltpu.SemaphoreType.DMA((2, rows, 2)),
            pltpu.SemaphoreType.DMA,
        ]
        self.peers = [("s", offset) for offset in range(1, rows)] + [("h", 1), ("c", 1)]

    def prepare(self, refs, place):
        self.source, self.target, self.along, self.across, self.core, self.local = refs
        self.place = place
        self.mine = place["s"] % 2 == place["c"]

    def row(self, offset):
        return flip(self.place["s"], offset)

    def along_copy(self, offset, arriving):
        to = self.row(offset)
        spot = to if arriving else self.place["s"]
        return remote(
            self.source.at[self.place["s"] // 2 if arriving else to // 2],
            self.target.at[spot, self.place["h"]],
            self.along.at[0, offset],
            self.along.at[1, offset],
            "s",
            offset,
        )

    def across_copy(self, offset, arriving):
        h = self.place["h"]
        own = self.target.at[self.row(offset), 1 - h if arriving else h]
        if offset == 0 and not arriving:
            source = self.source.at[self.place["s"] // 2]
        else:
            source = own
        return remote(source, own, self.across.at[0, offset], self.across.at[1, offset], "h", 1)

    def core_copy(self, offset, other):
        h = self.place["h"]
        own = self.target.at[self.row(offset), 1 - h if other else h]
        source = self.source.at[self.place["s"] // 2] if offset == 0 and not other else own
        return remote(source, own, self.core.at[0, offset, other], self.core.at[1, offset, other], "c", 1)

    def events(self):
        rows = self.sizes["s"]

        def first():
            for offset in range(1, rows):
                @pl.when(self.row(offset) % 2 == self.place["c"])
                def _():
                    self.along_copy(offset, False).start()

            @pl.when(self.mine)
            def _():
                pltpu.make_async_copy(
                    self.source.at[self.place["s"] // 2],
                    self.target.at[self.place["s"], self.place["h"]],
                    self.local,
                ).start()
                self.across_copy(0, False).start()
                self.core_copy(0, 0).start()

        def arrival(offset):
            @pl.when(self.mine)
            def _():
                self.along_copy(offset, True).wait_recv()
                self.across_copy(offset, False).start()
                self.core_copy(offset, 0).start()

        def other(offset):
            @pl.when(self.mine)
            def _():
                self.across_copy(offset, True).wait_recv()
                self.core_copy(offset, 1).start()

        found = [(0.05, first)]
        for offset in range(1, rows):
            found.append((offset + 0.05, functools.partial(arrival, offset)))
        for offset in range(rows):
            found.append((rows + offset, functools.partial(other, offset)))
        return found

    def finish(self):
        rows = self.sizes["s"]
        for offset in range(1, rows):
            @pl.when(self.row(offset) % 2 == self.place["c"])
            def _():
                self.along_copy(offset, False).wait_send()

        @pl.when(self.mine)
        def _():
            pltpu.make_async_copy(
                self.source.at[self.place["s"] // 2],
                self.target.at[self.place["s"], self.place["h"]],
                self.local,
            ).wait()
            for offset in range(rows):
                self.across_copy(offset, False).wait_send()
                for other in range(2):
                    self.core_copy(offset, other).wait_send()

        @pl.when(jnp.logical_not(self.mine))
        def _():
            for offset in range(rows):
                for other in range(2):
                    self.core_copy(offset, other).wait_recv()


class MemoryScatter:
    def __init__(self, value, sizes):
        self.value = value
        self.sizes = sizes
        rows = sizes["s"]
        self.block = value.shape[2:]
        self.out = jax.ShapeDtypeStruct((2,) + self.block, f32)
        self.in_spec = pl.BlockSpec(memory_space=pltpu.VMEM)
        self.out_spec = pl.BlockSpec(memory_space=pltpu.VMEM)
        self.scratch = [
            pltpu.VMEM(value.shape, value.dtype),
            pltpu.VMEM((rows,) + self.block, value.dtype),
            pltpu.VMEM((2,) + self.block, value.dtype),
            pltpu.SemaphoreType.DMA((2, rows, 2)),
            pltpu.SemaphoreType.DMA((2, rows)),
            pltpu.SemaphoreType.DMA((2, rows)),
        ]
        self.peers = [("s", offset) for offset in range(1, rows)] + [("h", 1), ("c", 1)]

    def prepare(self, refs, place):
        self.source, self.target = refs[0], refs[1]
        self.summed, self.halved, self.landed, self.core, self.across, self.along = refs[2:]
        self.place = place
        self.mine = place["s"] % 2 == place["c"]

    def row(self, offset):
        return flip(self.place["s"], offset)

    def core_copy(self, offset, other):
        h = self.place["h"]
        spot = (self.row(offset), flip(h, 1) if other else h)
        return remote(
            self.source.at[spot],
            self.summed.at[spot],
            self.core.at[0, offset, other],
            self.core.at[1, offset, other],
            "c",
            1,
        )

    def across_copy(self, offset):
        row = self.row(offset)
        return remote(
            self.summed.at[row, flip(self.place["h"], 1)],
            self.halved.at[row],
            self.across.at[0, offset],
            self.across.at[1, offset],
            "h",
            1,
        )

    def along_copy(self, offset, arriving):
        to = self.row(offset)
        return remote(
            self.halved.at[to],
            self.landed.at[to // 2 if arriving else self.place["s"] // 2],
            self.along.at[0, offset],
            self.along.at[1, offset],
            "s",
            offset,
        )

    def events(self):
        rows = self.sizes["s"]
        high, wide = self.block
        orders = list(range(1, rows))[::-1] + [0]

        def first():
            @pl.when(jnp.logical_not(self.mine))
            def _():
                for other in (1, 0):
                    for offset in orders:
                        self.core_copy(offset, other).start()

        def level(offset, other):
            @pl.when(self.mine)
            def _():
                self.core_copy(offset, other).wait_recv()
                h = self.place["h"]
                spot = (self.row(offset), flip(h, 1) if other else h)

                def body(piece):
                    total = self.summed[spot + (piece,)].astype(f32) + self.source[
                        spot + (piece,)
                    ].astype(f32)
                    self.summed[spot + (piece,)] = total.astype(self.summed.dtype)

                each_piece(high, wide, body)
                if other:
                    self.across_copy(offset).start()

        def last(offset):
            @pl.when(self.mine)
            def _():
                self.across_copy(offset).wait_recv()
                row = self.row(offset)

                def body(piece):
                    total = self.halved[(row, piece)].astype(f32) + self.summed[
                        (row, self.place["h"], piece)
                    ].astype(f32)
                    self.halved[(row, piece)] = total.astype(self.halved.dtype)
                    if offset == 0:
                        self.target[(self.place["s"] // 2, piece)] = total

                each_piece(high, wide, body)
                if offset:
                    self.along_copy(offset, False).start()

        found = [(-0.95, first)]
        for number, offset in enumerate(orders):
            found.append((0.05 + 0.1 * number, functools.partial(level, offset, 1)))
        for number, offset in enumerate(orders):
            found.append((0.55 + 0.1 * number, functools.partial(level, offset, 0)))
        for number, offset in enumerate(orders):
            found.append((1.05 + 0.2 * number, functools.partial(last, offset)))
        return found

    def finish(self):
        rows = self.sizes["s"]
        high, wide = self.block
        for offset in range(1, rows):
            @pl.when(self.row(offset) % 2 == self.place["c"])
            def _():
                self.along_copy(offset, True).wait_recv()
                number = self.row(offset) // 2

                def body(piece):
                    self.target[(number, piece)] = self.landed[(number, piece)].astype(f32)

                each_piece(high, wide, body)

        @pl.when(self.mine)
        def _():
            for offset in range(rows):
                self.across_copy(offset).wait_send()
            for offset in range(1, rows):
                self.along_copy(offset, False).wait_send()

        @pl.when(jnp.logical_not(self.mine))
        def _():
            for offset in range(rows):
                for other in range(2):
                    self.core_copy(offset, other).wait_send()


def exchange(name, collective_id, jobs):
    sizes = [len(job.scratch) for job in jobs]
    peers = []
    for job in jobs:
        for peer in job.peers:
            if peer not in peers:
                peers.append(peer)

    def kernel(*refs):
        count = len(jobs)
        scratch = refs[2 * count :]
        offset = 0
        barrier = pltpu.get_barrier_semaphore()
        for peer in peers:
            pl.semaphore_signal(
                barrier, inc=1, device_id=peer_of(*peer), device_id_type=pl.DeviceIdType.MESH
            )
        place = coordinates()
        for number, job in enumerate(jobs):
            job.prepare(
                (refs[number], refs[count + number]) + tuple(scratch[offset : offset + sizes[number]]),
                place,
            )
            offset += sizes[number]
        pl.semaphore_wait(barrier, len(peers))
        events = [event for job in jobs for event in job.events()]
        for _, act in sorted(events, key=lambda event: event[0]):
            act()
        for job in jobs:
            job.finish()

    return pl.pallas_call(
        kernel,
        name=name,
        out_shape=tuple(job.out for job in jobs),
        in_specs=[job.in_spec for job in jobs],
        out_specs=tuple(job.out_spec for job in jobs),
        scratch_shapes=[item for job in jobs for item in job.scratch],
        compiler_params=pltpu.CompilerParams(
            collective_id=collective_id, has_side_effects=True, vmem_limit_bytes=60 * 1024 * 1024
        ),
    )(*[job.value for job in jobs])


def packed(block):
    rows, columns = block.shape
    if rows % 16 == 0:
        return block
    return block.reshape(16, rows * columns // 16)


def bucket_edges():
    edges = []
    for target in range(1, 32):
        if target < 16:
            edges.append(target)
        else:
            found = 0
            for distance in range(16, 4096):
                value = 16 + int(math.log(distance / 16.0) / math.log(8.0) * 16.0)
                if found == 0 and value >= target:
                    found = distance
            edges.append(found)
    return edges


def bucket_of(distance):
    edges = jnp.array(bucket_edges(), dtype=jnp.int32)
    return jnp.sum((distance[..., None] >= edges).astype(jnp.int32), axis=-1)


def rms_norm(rows, gain):
    return rows * lax.rsqrt(jnp.mean(rows * rows, axis=-1, keepdims=True) + eps) * gain


def gelu_tanh(value):
    return (
        0.5
        * value
        * (1.0 + jnp.tanh(0.7978845608028654 * (value + 0.044715 * value * value * value)))
    )


def norm_back(rows, gain, slope):
    _, pullback = jax.vjp(rms_norm, rows, gain)
    return pullback(slope)


def dot(left, right):
    return jnp.einsum("sd,df->sf", left, right, preferred_element_type=f32)


def dot_t(left, right):
    return jnp.einsum("sf,df->sd", left, right, preferred_element_type=f32)


def t_dot(left, right):
    return jnp.einsum("sd,sf->df", left, right, preferred_element_type=f32)


def heads_of(tensor):
    return tensor.reshape(tensor.shape[0], HEADS, HEAD)


def attend_scores(query, keys, bias, mask):
    scores = jnp.einsum("qhe,khe->hqk", heads_of(query), heads_of(keys), preferred_element_type=f32)
    if bias is not None:
        scores = jnp.where(mask[None], scores + bias, masked_score)
    return scores


def attend(query, keys, values, bias, mask):
    scores = attend_scores(query, keys, bias, mask)
    highest = jnp.max(scores, axis=-1, keepdims=True)
    log_total = highest + jnp.log(jnp.sum(jnp.exp(scores - highest), axis=-1, keepdims=True))
    shares = jnp.exp(scores - log_total).astype(bf16)
    output = jnp.einsum("hqk,khe->qhe", shares, heads_of(values), preferred_element_type=f32)
    return output.reshape(query.shape).astype(bf16), log_total


def attend_back(query, keys, values, bias, mask, log_total, out_slope):
    scores = attend_scores(query, keys, bias, mask)
    shares = jnp.exp(scores - log_total)
    out_heads = heads_of(out_slope)
    share_slope = jnp.einsum("qhe,khe->hqk", out_heads, heads_of(values), preferred_element_type=f32)
    inner = jnp.sum(shares * share_slope, axis=-1, keepdims=True)
    score_slope = (shares * (share_slope - inner)).astype(bf16)
    query_slope = jnp.einsum("hqk,khe->qhe", score_slope, heads_of(keys), preferred_element_type=f32)
    key_slope = jnp.einsum("hqk,qhe->khe", score_slope, heads_of(query), preferred_element_type=f32)
    value_slope = jnp.einsum("hqk,qhe->khe", shares.astype(bf16), out_heads, preferred_element_type=f32)
    return (
        query_slope.reshape(query.shape).astype(bf16),
        jnp.concatenate(
            [key_slope.reshape(keys.shape), value_slope.reshape(values.shape)], axis=1
        ).astype(bf16),
        score_slope,
    )


def per_device(
    target_ids,
    labels,
    lengths,
    memory,
    embedding,
    head,
    gain_self,
    w_query,
    w_key,
    w_value,
    w_out,
    relative_bias,
    gain_cross,
    c_query,
    c_key,
    c_value,
    c_out,
    gain_ff,
    w_gate,
    w_up,
    w_down,
    gain_final,
):
    micro = target_ids.shape[0]
    seq_dev = target_ids.shape[2]
    mem_dev = memory.shape[2]
    voc_dev, width = embedding.shape
    ff = w_gate.shape[1]
    n_gx = lax.axis_size("gx")
    n_gy = lax.axis_size("gy")
    column = lax.axis_index("gy")
    row_group = lax.axis_index("gx")
    devices = n_gx * n_gy
    sizes = {"a": n_gx // 2, "c": 2, "s": n_gy // 2, "h": 2}
    assert sizes["s"] == 2 * micro
    place = coordinates()
    seq = seq_dev * n_gy
    plane = sizes["s"] * seq
    tok_dev = seq // 4
    span = sizes["a"] * voc_dev
    merged = "" if sizes["a"] == 2 else "ashc"

    gains = jnp.stack([gain_self, gain_cross, gain_ff, gain_final], axis=1)
    gains = jnp.pad(gains, ((0, 0), (0, GAIN_PAD - 4)))
    shards = (
        jnp.concatenate([w_gate, w_up], axis=1),
        jnp.concatenate([w_down, c_key, c_value, c_out], axis=1),
        jnp.concatenate([w_query, w_key, w_value, w_out, c_query, gains], axis=1),
    )
    orders = ("shac", "sahc", "sahc")
    own_ids = jnp.stack([target_ids.reshape(-1), labels.reshape(-1)])
    part_a, part_b, part_c, embed_rows, ids, memory_all = exchange(
        "gather_weights",
        0,
        [
            Gather(packed(part), order, "acsh", sizes, merged)
            for part, order in zip(shards, orders)
        ]
        + [
            Gather(embedding, "a", "a", sizes),
            Gather(own_ids, "shc", "shc", sizes, "shc"),
            MemoryGather(memory.reshape(micro, mem_dev, width), sizes),
        ],
    )
    part_a, part_b, part_c = (
        full.reshape(devices * part.shape[0], part.shape[1])
        for full, part in zip((part_a, part_b, part_c), shards)
    )
    embed_rows = embed_rows.reshape(span, width)
    memory_all = memory_all.reshape(n_gy * mem_dev, width)
    ids = ids.reshape(n_gy // 2, 2, 2, 2, micro, seq_dev).transpose(3, 4, 2, 0, 1, 5).reshape(2, plane)

    def local_of(index):
        shard = index // voc_dev
        held = (shard % n_gy == column) & (shard // n_gy % 2 == place["c"])
        return jnp.where(held, shard // (2 * n_gy) * voc_dev + index % voc_dev, -1)

    local_ids = local_of(ids[0])
    targets = local_of(ids[1])
    columns = jnp.arange(span, dtype=jnp.int32)
    norm_self, norm_cross, norm_ff, norm_final = (
        part_c[:, 5 * HD + number].astype(f32) for number in range(4)
    )
    qkv_w = part_c[:, : 3 * HD]
    self_out = part_c[:, 3 * HD : 4 * HD]
    cross_query = part_c[:, 4 * HD : 5 * HD]
    down_full = part_b[:, :ff]
    cross_kv = part_b[:, ff : ff + 2 * HD]
    cross_out = part_b[:, ff + 2 * HD :]

    picked_rows = dot((local_ids[:, None] == columns[None, :]).astype(bf16), embed_rows).astype(bf16)
    tok_layout = (sizes["s"], 2, 2, tok_dev, width)
    resid0, head_rows = exchange(
        "rows",
        1,
        [
            Scatter(picked_rows.reshape(tok_layout), "chs", "shc", sizes),
            Gather(head, "a", "a", sizes),
        ],
    )
    head_rows = head_rows.reshape(span, width)
    mem_kv = dot(memory_all, cross_kv).astype(bf16)
    keys_cross, values_cross = mem_kv[:, :HD], mem_kv[:, HD:]

    plane_lengths = lax.dynamic_slice_in_dim(lengths, 2 * place["a"], 2, axis=1).reshape(-1)
    live_length = lax.dynamic_index_in_dim(plane_lengths, place["s"], keepdims=False)
    query_pos = (2 * place["h"] + place["c"]) * tok_dev + jnp.arange(tok_dev, dtype=jnp.int32)
    key_pos = jnp.arange(seq, dtype=jnp.int32)
    bucket = bucket_of(jnp.maximum(query_pos[:, None] - key_pos[None, :], 0))
    indicator = (bucket[None] == jnp.arange(BUCKETS, dtype=jnp.int32)[:, None, None]).astype(bf16)
    bias = jnp.einsum("som,ns->nom", indicator, relative_bias, preferred_element_type=f32)
    mask = (key_pos[None, :] <= query_pos[:, None]) & (key_pos[None, :] < live_length)

    normed_self = rms_norm(resid0, norm_self).astype(bf16)
    qkv = dot(normed_self, qkv_w).astype(bf16)
    query_self = qkv[:, :HD]
    (self_kv_all,) = exchange("self_keys", 2, [Gather(qkv[:, HD:], "hc", "hc", sizes)])
    self_kv_all = self_kv_all.reshape(seq, 2 * HD)
    keys_self, values_self = self_kv_all[:, :HD], self_kv_all[:, HD:]
    attn_self, total_self = attend(query_self, keys_self, values_self, bias, mask)
    resid1 = resid0 + dot_t(attn_self, self_out)
    normed_cross = rms_norm(resid1, norm_cross).astype(bf16)
    query_cross = dot(normed_cross, cross_query).astype(bf16)
    attn_cross, total_cross = attend(query_cross, keys_cross, values_cross, None, None)
    resid2 = resid1 + dot_t(attn_cross, cross_out)
    normed_ff = rms_norm(resid2, norm_ff).astype(bf16)
    gate_up = dot(normed_ff, part_a)
    gate_value, up_value = gate_up[:, :ff], gate_up[:, ff:]
    hidden = (gelu_tanh(gate_value) * up_value).astype(bf16)
    resid3 = resid2 + dot_t(hidden, down_full)
    final_rows = rms_norm(resid3, norm_final).astype(bf16)

    (states,) = exchange("final_rows", 3, [Gather(final_rows, "shc", "shc", sizes, merged)])
    states = states.reshape(plane, width)
    logits = dot_t(states, head_rows)
    highest = jnp.max(logits, axis=1)
    own_total = highest + jnp.log(jnp.sum(jnp.exp(logits - highest[:, None]), axis=1))
    (totals,) = exchange(
        "totals", 4, [Gather(own_total.reshape(plane // 128, 128), "shc", "shc", sizes, merged)]
    )
    totals = totals.reshape(2 * n_gy, plane)
    top = jnp.max(totals, axis=0)
    log_total = top + jnp.log(jnp.sum(jnp.exp(totals - top[None]), axis=0))
    index = jnp.arange(plane, dtype=jnp.int32)
    alive = (index % seq < jnp.repeat(plane_lengths, seq)).astype(f32)
    hit = columns[None, :] == targets[:, None]
    picked = jnp.sum(jnp.where(hit, logits, 0.0), axis=1)
    loss_part = -jnp.sum(alive * picked) + jnp.where(
        (column == 0) & (place["c"] == 0), jnp.sum(alive * log_total), 0.0
    )
    slope = ((jnp.exp(logits - log_total[:, None]) - hit.astype(f32)) * alive[:, None]).astype(bf16)
    head_part = t_dot(slope, states).astype(bf16)
    final_part = dot(slope, head_rows).astype(bf16)
    final_slope, head_grad = exchange(
        "final_slopes",
        5,
        [
            Scatter(final_part.reshape(tok_layout), "chs", "shc", sizes),
            Scatter(head_part.reshape(sizes["a"], voc_dev, width), "a", "a", sizes),
        ],
    )

    grad3, norm_final_grad = norm_back(resid3, norm_final, final_slope)
    down_in = grad3.astype(bf16)
    down_grad = t_dot(down_in, hidden)
    hidden_slope = dot(down_in, down_full)
    activated, gelu_pull = jax.vjp(gelu_tanh, gate_value)
    up_slope = (hidden_slope * activated).astype(bf16)
    gate_slope = gelu_pull(hidden_slope * up_value)[0].astype(bf16)
    gate_up_slope = jnp.concatenate([gate_slope, up_slope], axis=1)
    gate_up_grad = t_dot(normed_ff, gate_up_slope)
    back_part, norm_ff_grad = norm_back(resid2, norm_ff, dot_t(gate_up_slope, part_a))
    grad2 = grad3 + back_part
    cross_in = grad2.astype(bf16)
    cross_out_grad = t_dot(cross_in, attn_cross)
    attn_slope = dot(cross_in, cross_out).astype(bf16)
    cross_query_slope, cross_kv_slope, _ = attend_back(
        query_cross, keys_cross, values_cross, None, None, total_cross, attn_slope
    )
    cross_query_grad = t_dot(normed_cross, cross_query_slope)
    cross_kv_grad = t_dot(memory_all, cross_kv_slope)
    memory_part = dot_t(cross_kv_slope, cross_kv).astype(bf16)
    back_part, norm_cross_grad = norm_back(
        resid1, norm_cross, dot_t(cross_query_slope, cross_query)
    )
    grad1 = grad2 + back_part
    self_in = grad1.astype(bf16)
    self_out_grad = t_dot(self_in, attn_self)
    attn_slope = dot(self_in, self_out).astype(bf16)
    query_slope, kv_slope, score_slope = attend_back(
        query_self, keys_self, values_self, bias, mask, total_self, attn_slope
    )
    bias_grad = jnp.einsum("noj,soj->ns", score_slope, indicator, preferred_element_type=f32)
    (kv_slope,) = exchange(
        "key_slopes",
        6,
        [Scatter(kv_slope.reshape(2, 2, tok_dev, 2 * HD), "ch", "hc", sizes, "", bf16)],
    )
    qkv_slope = jnp.concatenate([query_slope, kv_slope], axis=1)
    qkv_grad = t_dot(normed_self, qkv_slope)
    back_part, norm_self_grad = norm_back(resid0, norm_self, dot_t(qkv_slope, qkv_w))
    grad0 = grad1 + back_part
    (slopes,) = exchange("row_slopes", 7, [Gather(grad0.astype(bf16), "shc", "shc", sizes, merged)])
    embed_part = t_dot(
        (local_ids[:, None] == columns[None, :]).astype(bf16), slopes.reshape(plane, width)
    ).astype(bf16)
    gain_grads = jnp.stack([norm_self_grad, norm_cross_grad, norm_ff_grad, norm_final_grad], axis=1)
    gain_grads = jnp.pad(gain_grads, ((0, 0), (0, GAIN_PAD - 4)))
    sums = (
        gate_up_grad.astype(bf16),
        jnp.concatenate([down_grad, cross_kv_grad, cross_out_grad], axis=1).astype(bf16),
        jnp.concatenate([qkv_grad, self_out_grad, cross_query_grad, gain_grads], axis=1).astype(bf16),
    )
    small = jnp.concatenate([bias_grad.reshape(-1), loss_part[None]])
    small = jnp.pad(small, (0, 1024 - small.shape[0])).reshape(8, 128)
    device_layout = (sizes["a"], 2, sizes["s"], 2)
    blocks = [part.reshape(device_layout + packed_shape(part, devices)) for part in sums]
    grad_a, grad_b, grad_c, embedding_grad, memory_grad, small = exchange(
        "scatter_weights",
        8,
        [
            Scatter(part, order[::-1], "acsh", sizes, merged)
            for part, order in zip(blocks, orders)
        ]
        + [
            Scatter(embed_part.reshape(sizes["a"], voc_dev, width), "a", "a", sizes),
            MemoryScatter(memory_part.reshape(sizes["s"], 2, mem_dev, width), sizes),
            Gather(small, "shac", "acsh", sizes, "ashc"),
        ],
    )
    rows_dev = width // devices
    grad_a, grad_b, grad_c = (
        grad.reshape(rows_dev, part.shape[1]) for grad, part in zip((grad_a, grad_b, grad_c), sums)
    )
    small = jnp.sum(small.reshape(devices, 1024), axis=0)
    loss = small[HEADS * BUCKETS] / jnp.sum(lengths).astype(f32)
    bias_total = small[: HEADS * BUCKETS].reshape(HEADS, BUCKETS)
    gain_out = [grad_c[:, 5 * HD + number] for number in range(4)]
    return (
        loss,
        memory_grad.reshape(micro, 1, mem_dev, width),
        embedding_grad,
        head_grad,
        gain_out[0],
        grad_c[:, :HD],
        grad_c[:, HD : 2 * HD],
        grad_c[:, 2 * HD : 3 * HD],
        grad_c[:, 3 * HD : 4 * HD],
        bias_total,
        gain_out[1],
        grad_c[:, 4 * HD : 5 * HD],
        grad_b[:, ff : ff + HD],
        grad_b[:, ff + HD : ff + 2 * HD],
        grad_b[:, ff + 2 * HD :],
        gain_out[2],
        grad_a[:, :ff],
        grad_a[:, ff:],
        grad_b[:, :ff],
        gain_out[3],
    )


def packed_shape(part, count):
    rows, columns = part.shape[0] // count, part.shape[1]
    if rows % 16 == 0:
        return (rows, columns)
    return (16, rows * columns // 16)


def solution(mesh):
    placed = (
        P(None, "gx", "gy"),
        P(None, "gx", "gy"),
        P(),
        P(None, "gx", "gy", None),
        P(("gx", "gy"), None),
        P(("gx", "gy"), None),
        P(("gx", "gy")),
        P(("gx", "gy"), None),
        P(("gx", "gy"), None),
        P(("gx", "gy"), None),
        P(("gx", "gy"), None),
        P(),
        P(("gx", "gy")),
        P(("gx", "gy"), None),
        P(("gx", "gy"), None),
        P(("gx", "gy"), None),
        P(("gx", "gy"), None),
        P(("gx", "gy")),
        P(("gx", "gy"), None),
        P(("gx", "gy"), None),
        P(("gx", "gy"), None),
        P(("gx", "gy")),
    )
    return jax.shard_map(
        per_device,
        mesh=mesh,
        in_specs=placed,
        out_specs=(
            P(),
            P(None, "gx", "gy", None),
            P(("gx", "gy"), None),
            P(("gx", "gy"), None),
            P(("gx", "gy")),
            P(("gx", "gy"), None),
            P(("gx", "gy"), None),
            P(("gx", "gy"), None),
            P(("gx", "gy"), None),
            P(),
            P(("gx", "gy")),
            P(("gx", "gy"), None),
            P(("gx", "gy"), None),
            P(("gx", "gy"), None),
            P(("gx", "gy"), None),
            P(("gx", "gy")),
            P(("gx", "gy"), None),
            P(("gx", "gy"), None),
            P(("gx", "gy"), None),
            P(("gx", "gy")),
        ),
        check_vma=False,
    )
```

time: 503 us -> 435 us (0.86)
  Pallas kernels: 330 us -> 261 us
  matrix products: 66.4 us -> 80.6 us
  local copies, waits for them, and re-layouts: 54.2 us -> 45 us
  other arithmetic: 40 us -> 34.2 us
    pallas_call x9, Pallas kernels: 330 us -> 261 us  [exchange(): pl.pallas_call(kernel, name=name, out_shape=tuple((job.out for job in job...]
    concatenate x8 -> x4, local copies, waits for them, and re-layouts: 11.5 us -> 1.55 us  [attend_back(): jnp.concatenate([key_slope.reshape(keys.shape), value_slope.reshape(value...]
    dot_general x9, matrix products: 18.3 us -> 24.3 us  [dot(): return jnp.einsum('sd,df->sf', left, right, preferred_element_type=f32)]
    convert_element_type x2 -> x1, other arithmetic: 5.37 us -> 0.01 us  [per_device(): alive = (index % seq < jnp.repeat(plane_lengths, seq)).astype(f32)]
    unnamed x158 -> x169, local copies, waits for them, and re-layouts: 14.6 us -> 17.2 us
where the time goes in v2:
time: 435 us; the launch traced here: 426 us
  Pallas kernels  261 us (60%)
  matrix products  80.6 us (19%)
  local copies, waits for them, and re-layouts  45 us (10%)
  other arithmetic  34.2 us (8%)
  between operations  6.11 us (1%)
    pallas_call x9, Pallas kernels, exchange(): pl.pallas_call(kernel, name=name, out_shape=tuple((job.out for job in job...  261 us
    dot_general x9, matrix products, dot(): return jnp.einsum('sd,df->sf', left, right, preferred_element_type=f32)  24.3 us
    dot_general x9, matrix products, t_dot(): return jnp.einsum('sd,sf->df', left, right, preferred_element_type=f32)  19.5 us
    dot_general x8, matrix products, dot_t(): return jnp.einsum('sf,df->sd', left, right, preferred_element_type=f32)  18.3 us
    unnamed x169, local copies, waits for them, and re-layouts  17.2 us

profile of v2, /device:TPU:0, one launch (start us, length us, event | category | flops | bytes accessed | tf_op | source)
XLA Modules:
  0.0 426.4 jit_solution(15217545204661261740)
XLA Ops:
  1.2 1.3 reduce.26
  2.6 1.3 reduce.25
  9.0 1.5 pad_maximum_fusion.12.refs_1_
  10.5 1.4 pad_maximum_fusion.13.refs_0_
  11.9 54.5 %gather_weights.1 = (bf16[2,2,4,2,16,2048]{5,4,3,2,1,0:T(8,128)(2,1)}, bf16[2,2,4,2,16,2176]{5,4,3,2,1,0:T(8,128)(2,1)}, bf16[2,2,4,2,16,2048]{5,4,3,2,1,0:T(8,1...) custom-call(bf16[16,2048]{1,0:T(8,128)(2,1)} %pad_maximum_fusion.13.refs_0_, ...), custom_call_target="tpu_custom_call" | custom-call | tf_op jit(solution)/shard_map/gather_weights/pallas_call | solution.py:607
  68.1 4.8 %fusion.8 = bf16[2048,512]{1,0:T(8,128)(2,1)} fusion(bf16[1024,512]{1,0:T(8,128)(2,1)} %bitcast.247, s32[2048]{0:T(1024)S(1)} %get-tuple-element.194), kind=kOutput, calls=%fused_computation.19 | convolution fusion | flops 2150629376 | bytes 3153920 | tf_op jit(solution)/shard_map/sd,df->sf/dot_general | solution.py:665
  72.9 25.4 %rows.1 = (f32[128,512]{1,0:T(8,128)}, bf16[2,512,512]{2,1,0:T(8,128)(2,1)}) custom-call(bf16[4,2,2,128,512]{4,3,2,1,0:T(8,128)(2,1)} %bitcast.181, bf16[512,512]{1,0:T(8,128)(2,1)} %refs_1_.1), custom_call_target="tpu_custom_call" | custom-call | tf_op jit(solution)/shard_map/rows/pallas_call | solution.py:607
  98.3 1.1 multiply_reduce_fusion.13
  99.5 1.1 slice_convert_fusion
  101.8 9.6 %self_keys.1 = bf16[2,2,128,768]{3,2,1,0:T(8,128)(2,1)} custom-call(bf16[128,768]{1,0:T(8,128)(2,1)} %slice.159.refs_0_), custom_call_target="tpu_custom_call" | custom-call | tf_op jit(solution)/shard_map/self_keys/pallas_call | solution.py:607
  111.4 1.2 fusion.105
  112.8 1.0 slice.161
  117.3 1.3 fusion.1
  118.7 1.8 copy.140
  120.5 1.9 fusion.110
  123.7 1.4 multiply_reduce_fusion.12
  125.3 1.3 convolution_convert_fusion.21
  126.7 2.5 convolution_convert_fusion.4
  133.2 2.0 multiply_reduce_fusion.11
  135.2 1.1 copy.178
  136.3 2.2 fusion.101
  138.8 2.7 multiply_reduce_fusion.10
  141.4 1.1 copy.179
  142.5 1.7 multiply_convert_fusion.5.refs_0_
  144.2 22.0 %final_rows.1 = bf16[4,2,2,128,512]{4,3,2,1,0:T(8,128)(2,1)} custom-call(bf16[128,512]{1,0:T(8,128)(2,1)} %multiply_convert_fusion.5.refs_0_), custom_call_target="tpu_custom_call" | custom-call | tf_op jit(solution)/shard_map/final_rows/pallas_call | solution.py:607
  166.2 4.2 fusion.112
  170.4 2.7 select_reduce_fusion
  174.2 11.9 %totals.1 = f32[4,2,2,16,128]{4,3,2,1,0:T(8,128)} custom-call(f32[16,128]{1,0:T(8,128)} %add_bitcast_fusion.1.refs_0_), custom_call_target="tpu_custom_call" | custom-call | tf_op jit(solution)/shard_map/totals/pallas_call | solution.py:607
  191.0 7.5 %convolution_convert_fusion.7 = bf16[1024,512]{1,0:T(8,128)(2,1)} fusion(bf16[2048,512]{1,0:T(8,128)(2,1)} %bitcast.186, f32[2048,1024]{0,1:T(8,128)} %copy-done.7, f32[2048]{0:T(1024)S(1)} %fusion.80, s32[2048]{0:T(1024)S(1)} %get-tuple-element.195, f32[2048]{0:T(1024)S(1)} %get-tuple-element.174), kind=kOutput, calls=%fused_computation.40 | convolution fusion | flops 2160590848 | bytes 11558912 | tf_op jit(solution)/shard_map/sd,sf->df/dot_general | solution.py:673
  198.5 7.6 %convolution_convert_fusion.1 = bf16[2048,512]{1,0:T(8,128)(2,1)} fusion(bf16[1024,512]{1,0:T(8,128)(2,1)S(1)} %bitcast.246, f32[2048,1024]{0,1:T(8,128)} %copy-done.7, f32[2048]{0:T(1024)S(1)} %fusion.80, s32[2048]{0:T(1024)S(1)} %get-tuple-element.195, f32[2048]{0:T(1024)S(1)} %get-tuple-element.174), kind=kOutput, calls=%fused_computation.21 | convolution fusion | flops 2161115136 | bytes 11558912 | tf_op jit(solution)/shard_map/sd,df->sf/dot_general | solution.py:665
  206.1 33.3 %final_slopes.1 = (f32[128,512]{1,0:T(8,128)}, f32[512,512]{1,0:T(8,128)}) custom-call(bf16[4,2,2,128,512]{4,3,2,1,0:T(8,128)(2,1)} %bitcast.182, bf16[2,512,512]{2,1,0:T(8,128)(2,1)} %bitcast.194), custom_call_target="tpu_custom_call" | custom-call | tf_op jit(solution)/shard_map/final_slopes/pallas_call | solution.py:607
  239.4 1.1 multiply_reduce_fusion.3
  240.5 1.1 add_add_fusion.3
  241.6 2.3 fusion.32
  246.4 1.9 convolution_convert_fusion.19
  249.3 2.1 multiply_reduce_fusion
  253.2 1.4 multiply_reduce_fusion.7
  256.2 1.2 convolution_convert_fusion.17
  257.6 2.2 multiply_reduce_fusion.1
  259.8 1.2 multiply_convert_fusion.2
  261.1 2.5 copy.160
  263.6 2.9 fusion.20
  267.3 2.7 convolution_convert_fusion.9
  270.0 2.3 copy.147
  272.3 1.6 convolution_convert_fusion.8
  273.9 1.5 copy.148
  275.4 3.7 convolution_convert_fusion.5
  283.0 10.6 %key_slopes.1 = bf16[128,768]{1,0:T(8,128)(2,1)} custom-call(bf16[2,2,128,768]{3,2,1,0:T(8,128)(2,1)} %pad_maximum_fusion.5.refs_0_), custom_call_target="tpu_custom_call" | custom-call | tf_op jit(solution)/shard_map/key_slopes/pallas_call | solution.py:607
  293.7 2.0 multiply_reduce_fusion.2
  296.5 21.6 %row_slopes.1 = bf16[4,2,2,128,512]{4,3,2,1,0:T(8,128)(2,1)} custom-call(bf16[128,512]{1,0:T(8,128)(2,1)} %fusion.48.refs_0_), custom_call_target="tpu_custom_call" | custom-call | tf_op jit(solution)/shard_map/row_slopes/pallas_call | solution.py:607
  318.2 5.4 %fusion.13 = bf16[1024,512]{1,0:T(8,128)(2,1)} fusion(bf16[2048,512]{1,0:T(8,128)(2,1)} %bitcast.187, s32[2048]{0:T(1024)S(1)} %copy-done.59), kind=kOutput, calls=%fused_computation.39 | convolution fusion | flops 2150105088 | bytes 3153920 | tf_op jit(solution)/shard_map/sd,sf->df/dot_general | solution.py:673
  325.3 1.6 pad_maximum_fusion.1.refs_2_
  328.1 1.5 copy.145
  329.7 2.7 fusion.14
  332.8 1.5 pad_maximum_fusion.refs_1_
  334.4 2.1 convolution_convert_fusion
  336.5 71.8 %scatter_weights.1 = (f32[16,2048]{1,0:T(8,128)}, f32[16,2176]{1,0:T(8,128)}, f32[16,2048]{1,0:T(8,128)}, f32[512,512]{1,0:T(8,128)}, f32[2,128,512]{2,1,0:T(8,128)}, /*index=5*/f32[2,2,4,2,8,128]{5,4,3,2,1,0:T(8,128)}) custom-call(bf16[2,2,4,2,16,2048]{5,4,3,2,1,0:T(8,128)(2,1)} %bitcast.160, bf16[2,2,4,2,16,2176]{5,4,3,2,1,0:T(8,128)(2,1)} %pad_maximum_fusion.refs_1_, ...), custom_call_target="tpu_custom_call" | custom-call | tf_op jit(solution)/shard_map/scatter_weights/pallas_call | solution.py:607
  408.3 1.6 fusion.107
  409.9 1.5 fusion.108
  411.4 1.4 fusion.106
  412.8 1.5 slice.154
  418.4 1.6 slice_reduce_fusion
  420.0 1.9 copy.190
  421.8 2.3 copy.191
  (260 shorter events, 41.6 us)
Async XLA Ops:
  0.7 116.7 %copy-start = (bf16[6,32]{1,0:T(8,128)(2,1)S(1)}, bf16[6,32]{1,0:T(8,128)(2,1)}, u32[]{:S(2)}) copy-start(bf16[6,32]{1,0:T(8,128)(2,1)} %param.34) | copy-start | bytes 1156
  9.0 2.9 copy-start.57
  72.9 26.6 %copy-start.29 = (bf16[2,2,4,2,16,2048]{5,4,3,2,1,0:T(8,128)(2,1)S(1)}, bf16[2,2,4,2,16,2048]{5,4,3,2,1,0:T(8,128)(2,1)}, u32[]{:S(2)}) copy-start(bf16[2,2,4,2,16,2048]{5,4,3,2,1,0:T(8,128)(2,1)} %get-tuple-element.39) | copy-start | bytes 6291460
  98.3 2.4 copy-start.15
  99.4 11.9 %copy-start.72 = (f32[128]{0:T(128)}, f32[128]{0:T(128)S(1)}, u32[]{:S(2)}) copy-start(f32[128]{0:T(128)S(1)} %multiply_reduce_fusion.13) | copy-start | bytes 1540
  99.5 11.9 %copy-start.66 = (f32[128]{0:T(128)}, f32[128]{0:T(128)S(1)}, u32[]{:S(2)}) copy-start(f32[128]{0:T(128)S(1)} %fusion.90) | copy-start | bytes 1540
  101.1 11.5 %copy-start.52 = (bf16[128,1152]{1,0:T(8,128)(2,1)}, bf16[128,1152]{1,0:T(8,128)(2,1)S(1)}, u32[]{:S(2)}) copy-start(bf16[128,1152]{1,0:T(8,128)(2,1)S(1)} %convolution_convert_fusion.3) | copy-start | bytes 884740
  101.1 12.9 %copy-start.64 = (s32[2,4]{1,0:T(2,128)S(1)}, s32[2,4]{1,0:T(2,128)}, u32[]{:S(2)}) copy-start(s32[2,4]{1,0:T(2,128)} %param.25) | copy-start | bytes 100
  101.8 14.5 %copy-start.74 = (s32[31]{0:T(128)S(1)}, s32[31]{0:T(128)}, u32[]{:S(2)}) copy-start(s32[31]{0:T(128)} %constant.198.clone) | copy-start | bytes 376
  112.8 7.7 %copy-start.19 = (bf16[512,384]{0,1:T(8,128)(2,1)}, bf16[512,384]{0,1:T(8,128)(2,1)S(1)}, u32[]{:S(2)}) copy-start(bf16[512,384]{0,1:T(8,128)(2,1)S(1)} %copy.138) | copy-start | bytes 1179652
  114.0 6.6 %copy-start.45 = (bf16[128,384]{0,1:T(8,128)(2,1)}, bf16[128,384]{0,1:T(8,128)(2,1)S(1)}, u32[]{:S(2)}) copy-start(bf16[128,384]{0,1:T(8,128)(2,1)S(1)} %copy.137) | copy-start | bytes 294916
  117.3 3.2 copy-start.34
  123.0 2.2 copy-start.33
  123.2 3.5 copy-start.18
  123.7 5.5 %copy-start.36 = (bf16[6,64,128]{2,1,0:T(8,128)(2,1)}, bf16[6,64,128]{2,1,0:T(8,128)(2,1)S(1)}, u32[]{:S(2)}) copy-start(bf16[6,64,128]{2,1,0:T(8,128)(2,1)S(1)} %convolution_convert_fusion.16) | copy-start | bytes 294916
  125.1 4.1 copy-start.70
  125.1 4.1 copy-start.60
  126.7 2.7 copy-start.40
  129.4 2.4 copy-start.10
  135.2 109.7 %copy-start.62 = (f32[128]{0:T(128)}, f32[128]{0:T(128)S(1)}, u32[]{:S(2)}) copy-start(f32[128]{0:T(128)S(1)} %fusion.92) | copy-start | bytes 1540
  136.3 2.4 copy-start.11
  138.5 2.9 copy-start.14
  138.7 2.7 copy-start.21
  170.4 3.2 copy-start.7
  170.4 17.6 %copy-start.69 = (s32[4]{0:T(128)S(1)}, s32[4]{0:T(128)}, u32[]{:S(2)}) copy-start(s32[4]{0:T(128)} %copy-done.68) | copy-start | bytes 52
  191.0 7.5 %copy-start.75 = (bf16[2,512,512]{2,1,0:T(8,128)(2,1)S(1)}, bf16[2,512,512]{2,1,0:T(8,128)(2,1)}, u32[]{:S(2)}) copy-start(bf16[2,512,512]{2,1,0:T(8,128)(2,1)} %get-tuple-element.43) | copy-start | bytes 3145732
  206.1 33.3 %copy-start.17 = (f32[128,512]{1,0:T(8,128)S(1)}, f32[128,512]{1,0:T(8,128)}, u32[]{:S(2)}) copy-start(f32[128,512]{1,0:T(8,128)} %get-tuple-element.184) | copy-start | bytes 786436
  241.5 3.4 copy-start.27
  241.6 2.4 copy-start.12
  241.6 2.4 copy-start.30
  243.9 1.8 copy-start.53
  243.9 1.8 copy-start.55
  252.5 3.0 copy-start.5
  252.5 2.1 copy-start.71
  252.5 2.1 copy-start.26
  253.2 2.3 copy-start.38
  257.6 2.2 copy-start.41
  257.6 2.2 copy-start.3
  259.8 3.8 copy-start.35
  275.4 3.8 copy-start.47
  275.4 3.8 copy-start.6
  275.4 3.8 copy-start.20
  275.4 4.3 %copy-start.46 = (bf16[128,384]{0,1:T(8,128)(2,1)S(1)}, bf16[128,384]{0,1:T(8,128)(2,1)}, u32[]{:S(2)}) copy-start(bf16[128,384]{0,1:T(8,128)(2,1)} %copy-done.45) | copy-start | bytes 294916
  279.2 1.6 copy-start.4
  279.2 1.6 copy-start.42
  281.3 12.4 %copy-start.16 = (f32[128,512]{1,0:T(8,128)S(1)}, f32[128,512]{1,0:T(8,128)}, u32[]{:S(2)}) copy-start(f32[128,512]{1,0:T(8,128)} %get-tuple-element.38) | copy-start | bytes 786436
  281.3 12.4 %copy-start.67 = (f32[128]{0:T(128)S(1)}, f32[128]{0:T(128)}, u32[]{:S(2)}) copy-start(f32[128]{0:T(128)} %copy-done.66) | copy-start | bytes 1540
  283.0 12.7 %copy-start.73 = (f32[128]{0:T(128)S(1)}, f32[128]{0:T(128)}, u32[]{:S(2)}) copy-start(f32[128]{0:T(128)} %copy-done.72) | copy-start | bytes 1540
  283.0 12.7 %copy-start.24 = (f32[128,512]{1,0:T(8,128)S(1)}, f32[128,512]{1,0:T(8,128)}, u32[]{:S(2)}) copy-start(f32[128,512]{1,0:T(8,128)} %copy-done.23) | copy-start | bytes 786436
  295.7 22.4 %copy-start.59 = (s32[2048]{0:T(1024)S(1)}, s32[2048]{0:T(1024)}, u32[]{:S(2)}) copy-start(s32[2048]{0:T(1024)} %copy-done.58) | copy-start | bytes 24580
  318.1 5.5 %copy-start.48 = (bf16[128,768]{1,0:T(8,128)(2,1)S(1)}, bf16[128,768]{1,0:T(8,128)(2,1)}, u32[]{:S(2)}) copy-start(bf16[128,768]{1,0:T(8,128)(2,1)} %key_slopes.1) | copy-start | bytes 589828
  318.1 6.0 %copy-start.50 = (bf16[512,128]{0,1:T(8,128)(2,1)S(1)}, bf16[512,128]{0,1:T(8,128)(2,1)}, u32[]{:S(2)}) copy-start(bf16[512,128]{0,1:T(8,128)(2,1)} %get-tuple-element.146) | copy-start | bytes 393220
  318.1 6.1 %copy-start.37 = (bf16[6,64,128]{2,1,0:T(8,128)(2,1)S(1)}, bf16[6,64,128]{2,1,0:T(8,128)(2,1)}, u32[]{:S(2)}) copy-start(bf16[6,64,128]{2,1,0:T(8,128)(2,1)} %copy-done.36) | copy-start | bytes 294916
  325.3 1.6 copy-start.22
  325.3 1.6 copy-start.28
  329.6 2.7 copy-start.51
  329.6 2.9 copy-start.44
  332.8 1.6 copy-start.13
  332.8 1.6 copy-start.54
  332.8 1.6 copy-start.56
  332.8 1.6 copy-start.63
  336.5 79.9 %copy-start.65 = (s32[2,4]{1,0:T(2,128)S(1)}, s32[2,4]{1,0:T(2,128)}, u32[]{:S(2)}) copy-start(s32[2,4]{1,0:T(2,128)} %param.25) | copy-start | bytes 100
  408.3 15.8 %copy-start.32 = (f32[512,512]{1,0:T(8,128)S(1)}, f32[512,512]{1,0:T(8,128)}, u32[]{:S(2)}) copy-start(f32[512,512]{1,0:T(8,128)} %get-tuple-element.219) | copy-start | bytes 3145732
  420.0 5.1 %copy-start.1 = (bf16[6,32]{1,0:T(8,128)(2,1)S(1)}, bf16[6,32]{1,0:T(8,128)(2,1)}, u32[]{:S(2)}) copy-start(bf16[6,32]{1,0:T(8,128)(2,1)} %param.34) | copy-start | bytes 1156
  (12 other events, 11.2 us)
